TPU v7x, 32 devices: a whole 2x2x4 slice. The times are simulated.
32 devices in a mesh: groups: 2 (over x), replica: 8 (over z, y), channel: 2 (over core).
Axes of the slice: x: 2, y: 2, z: 4, core: 2. Of those that a mesh axis runs over, the one named last changes fastest.
Arguments:
- queries: bfloat16 [16, 2, 32, 4096], P(('groups', 'replica'), None, None, 'channel'), parts along dimension 0, may hold values from -360 to 360
- new_kv: bfloat16 [16, 2, 32, 1024], P(('groups', 'replica'), None, None, 'channel'), parts along dimension 0, may hold values from -6 to 6
- cached_lookup_pairs: bfloat16 [16, 1024, 1024], P(('groups', 'replica'), None, 'channel'), parts along dimension 0, may hold values from -6 to 6
- prefix_ssm: bfloat16 [16, 16, 8192], P(('groups', 'replica'), None, 'channel'), parts along dimension 0, may hold values from -6 to 6
- prefix_conv: bfloat16 [16, 3, 8192], P(('groups', 'replica'), None, 'channel'), parts along dimension 0, may hold values from -6 to 6
- pool_kv: bfloat16 [16, 4, 256, 1024], P(('groups', 'replica'), None, None, 'channel'), parts along dimension 0, may hold values from -6 to 6
- pool_ssm: bfloat16 [16, 16, 8192], P(('groups', 'replica'), None, 'channel'), parts along dimension 0, may hold values from -6 to 6
- pool_conv: bfloat16 [16, 3, 8192], P(('groups', 'replica'), None, 'channel'), parts along dimension 0, may hold values from -6 to 6
- owner_id: int32 [2], P('groups'), parts along dimension 0, may hold values from 0 to 7
- readers: int32 [16], P(('groups', 'replica')), parts along dimension 0, may hold values 0 or 1
- restore_src: int32 [16, 4], P('groups'), parts along dimension 0, may hold values from 0 to 7, as said below
- restore_blk: int32 [16, 4], P('groups'), parts along dimension 0, may hold values from 0 to 3, as said below
- state_src: int32 [16], P('groups'), parts along dimension 0, may hold values from 0 to 7, as said below
- ctx_blocks: int32 [16], P(('groups', 'replica')), parts along dimension 0, may hold values from 1 to 4, as said below
- mamba_x: bfloat16 [16, 2, 32, 8192], P(('groups', 'replica'), None, None, 'channel'), parts along dimension 0, may hold values from -6 to 6
- mamba_z: bfloat16 [16, 2, 32, 8192], P(('groups', 'replica'), None, None, 'channel'), parts along dimension 0, may hold values from -6 to 6
- mamba_dt: bfloat16 [16, 2, 32, 8192], P(('groups', 'replica'), None, None, 'channel'), parts along dimension 0, may hold values from -2 to 8
- dt_bias: float32 [8192], P('channel'), may hold values from -6 to -2.5
- a_log: float32 [16, 8192], P(None, 'channel'), may hold values from 0 to 2
- bypass_gain: float32 [8192], P('channel'), may hold values from 0.5 to 1.5
- conv_w: float32 [4, 8192], P(None, 'channel'), may hold values from -3 to 3
- conv_b: float32 [8192], P('channel'), may hold values from -0.5 to 0.5
- w_bc: bfloat16 [8192, 32], P('channel'), may hold values from -0.0625 to 0.0625
Outputs:
- attention_out: bfloat16 [16, 2, 32, 4096], P(('groups', 'replica'), None, None, 'channel'), parts along dimension 0
- mamba_out: bfloat16 [16, 2, 32, 8192], P(('groups', 'replica'), None, None, 'channel'), parts along dimension 0
There are 2 independent parts, one for each index of `groups`. A program takes and returns all parts, laid end to end along the dimension named above; an argument that names none is the same for every part. Nothing has to cross between parts.
Inputs may be any that keep to these rules, and one draw needn't show every extreme that they name: `restore_src`: each row names 4 different replicas, and each replica is named in exactly 4 rows, so at most one block goes from one replica to one row's replica. Every pair (restore_src, restore_blk) is different: each stored block of each replica is listed exactly once. `state_src`: A permutation of the replicas. Only slots j < ctx_blocks[d] of row d are read; some replica has 4.
All inputs are finite; a program needn't handle non-finite values. No bound on the sum of `readers` on one device may be relied on, other than what follows from the above.
Results may differ from a plain program's by a relative error of at most 0.0049.
Values may be sent and summed in bfloat16 or wider, within the bound.
A program may use at most 128 MiB of HBM per device.

v0:
```python
import jax
import jax.numpy as jnp
from jax import lax
from jax.experimental import pallas as pl
from jax.experimental.pallas import tpu as pltpu
from jax.sharding import PartitionSpec as P

HD = 128
Q_PER_KV = 8
CHUNK = 512


def from_root(value, axis, source):
    kept = jnp.where(lax.axis_index(axis) == source, value, 0).astype(value.dtype)
    return lax.psum(kept, axis)


def attend_kernel(parts, src_ref, live_ref, q_ref, *refs):
    ctx_refs, new_ref, out_ref = refs[:parts], refs[parts], refs[parts + 1]
    new_len = q_ref.shape[0]
    heads = new_ref.shape[1] // (2 * HD)
    factor = HD ** (-0.5)
    rows = Q_PER_KV * new_len
    live = live_ref[0]
    for head in range(heads):
        query = jnp.concatenate(
            [
                q_ref[:, (head * Q_PER_KV + g) * HD : (head * Q_PER_KV + g + 1) * HD]
                for g in range(Q_PER_KV)
            ],
            axis=0,
        )
        key_cols = slice(2 * head * HD, (2 * head + 1) * HD)
        value_cols = slice((2 * head + 1) * HD, (2 * head + 2) * HD)
        contract = (((1,), (1,)), ((), ()))
        scores = []
        start = 0
        for ref in ctx_refs:
            piece = (
                lax.dot_general(
                    query, ref[0, :, key_cols], contract, preferred_element_type=jnp.float32
                )
                * factor
            )
            position = start + lax.broadcasted_iota(jnp.int32, piece.shape, 1)
            scores.append(jnp.where(position < live, piece, -jnp.inf))
            start += ref.shape[1]
        fresh = (
            lax.dot_general(
                query, new_ref[:, key_cols], contract, preferred_element_type=jnp.float32
            )
            * factor
        )
        time = lax.rem(lax.broadcasted_iota(jnp.int32, fresh.shape, 0), new_len)
        fresh = jnp.where(
            time >= lax.broadcasted_iota(jnp.int32, fresh.shape, 1), fresh, -jnp.inf
        )
        highest = jnp.max(fresh, axis=1, keepdims=True)
        for piece in scores:
            highest = jnp.maximum(highest, jnp.max(piece, axis=1, keepdims=True))
        weight = jnp.exp(fresh - highest)
        total = jnp.sum(weight, axis=1, keepdims=True)
        mixed = jnp.dot(
            weight.astype(jnp.bfloat16),
            new_ref[:, value_cols],
            preferred_element_type=jnp.float32,
        )
        for piece, ref in zip(scores, ctx_refs):
            weight = jnp.exp(piece - highest)
            total = total + jnp.sum(weight, axis=1, keepdims=True)
            mixed = mixed + jnp.dot(
                weight.astype(jnp.bfloat16),
                ref[0, :, value_cols],
                preferred_element_type=jnp.float32,
            )
        result = (mixed / total).astype(out_ref.dtype)
        for g in range(Q_PER_KV):
            at = (head * Q_PER_KV + g) * HD
            out_ref[:, at : at + HD] = result[g * new_len : (g + 1) * new_len]


def attend(request, queries, blocks, source, live, new_kv):
    parts = source.shape[0]
    _, block_len, width = blocks.shape
    _, _, new_len, q_width = queries.shape

    def pick(j):
        return pl.BlockSpec((1, block_len, width), lambda i, s, l: (s[j], 0, 0))

    return pl.pallas_call(
        lambda *refs: attend_kernel(parts, *refs),
        grid_spec=pltpu.PrefetchScalarGridSpec(
            num_scalar_prefetch=2,
            grid=(1,),
            in_specs=[
                pl.BlockSpec((None, None, new_len, q_width), lambda i, s, l: (0, request, 0, 0))
            ]
            + [pick(j) for j in range(parts)]
            + [pl.BlockSpec((None, None, new_len, width), lambda i, s, l: (0, request, 0, 0))],
            out_specs=pl.BlockSpec((new_len, q_width), lambda i, s, l: (0, 0)),
        ),
        out_shape=jax.ShapeDtypeStruct((new_len, q_width), jnp.bfloat16),
        name="attend",
    )(source, live, queries, *([blocks] * parts), new_kv)


def signal_kernel(read_ref, x_ref, conv0_ref, conv1_ref, w_ref, b_ref, wbc_ref, sig_ref, bc_ref, pad):
    taps = w_ref.shape[0]
    new_len = x_ref.shape[1]
    reading = read_ref[0] > 0
    base = 8 - (taps - 1)
    first = jnp.where(reading, conv0_ref[...].astype(jnp.float32), 0.0)
    pad[0, base:8] = first
    pad[1, base:8] = conv1_ref[...].astype(jnp.float32)

    @pl.when(pl.program_id(0) == 0)
    def _():
        bc_ref[...] = jnp.zeros_like(bc_ref)

    for r in range(2):
        pad[r, 8 : 8 + new_len] = x_ref[r].astype(jnp.float32)
        total = b_ref[...] + w_ref[0:1] * pad[r, base : base + new_len]
        for k in range(1, taps):
            total = total + w_ref[k : k + 1] * pad[r, base + k : base + k + new_len]
        signal = total * jax.nn.sigmoid(total)
        sig_ref[r] = signal
        bc_ref[r] += jnp.dot(
            signal.astype(jnp.bfloat16), wbc_ref[...], preferred_element_type=jnp.float32
        )


def signal_call(reading, x, conv0, conv1, w, b, wbc):
    _, _, new_len, channels = x.shape
    taps, cols = w.shape[0], wbc.shape[1]
    chunk = CHUNK
    return pl.pallas_call(
        signal_kernel,
        grid_spec=pltpu.PrefetchScalarGridSpec(
            num_scalar_prefetch=1,
            grid=(channels // chunk,),
            in_specs=[
                pl.BlockSpec((None, 2, new_len, chunk), lambda i, s: (0, 0, 0, i)),
                pl.BlockSpec((taps - 1, chunk), lambda i, s: (0, i)),
                pl.BlockSpec((taps - 1, chunk), lambda i, s: (0, i)),
                pl.BlockSpec((taps, chunk), lambda i, s: (0, i)),
                pl.BlockSpec((1, chunk), lambda i, s: (0, i)),
                pl.BlockSpec((chunk, cols), lambda i, s: (i, 0)),
            ],
            out_specs=[
                pl.BlockSpec((2, new_len, chunk), lambda i, s: (0, 0, i)),
                pl.BlockSpec((2, new_len, cols), lambda i, s: (0, 0, 0)),
            ],
            scratch_shapes=[pltpu.VMEM((2, 8 + new_len, chunk), jnp.float32)],
        ),
        out_shape=[
            jax.ShapeDtypeStruct((2, new_len, channels), jnp.float32),
            jax.ShapeDtypeStruct((2, new_len, cols), jnp.float32),
        ],
        name="signal",
    )(reading, x, conv0, conv1, w, b, wbc)


def scan_kernel(
    read_ref, bc_ref, sig_ref, dt_ref, z_ref, bias_ref, alog_ref, gain_ref, s0_ref, s1_ref,
    out_ref, spread, step_buf, push_buf, scan_buf
):
    states, chunk = alog_ref.shape
    new_len = sig_ref.shape[1]

    @pl.when(pl.program_id(0) == 0)
    def _():
        for r in range(2):
            columns = bc_ref[r].T
            for t in range(new_len):
                spread[r, t] = jnp.broadcast_to(columns[:, t : t + 1], spread.shape[2:])

    decay = -jnp.exp(alog_ref[...])
    hidden = []
    for r in range(2):
        x = dt_ref[r].astype(jnp.float32) + bias_ref[...]
        step = jnp.maximum(x, 0.0) + jnp.log1p(jnp.exp(-jnp.abs(x)))
        step_buf[r] = step
        push_buf[r] = step * sig_ref[r]
    hidden = (
        jnp.where(read_ref[0] > 0, s0_ref[...].astype(jnp.float32), 0.0),
        s1_ref[...].astype(jnp.float32),
    )
    tiles = chunk // HD
    for t in range(new_len):
        state = []
        for r in range(2):
            now = jnp.broadcast_to(step_buf[r, t : t + 1], (states, chunk))
            push = jnp.broadcast_to(push_buf[r, t : t + 1], (states, chunk))
            both = spread[r, t]
            gain = jnp.concatenate([both[:states]] * tiles, axis=1)
            read = jnp.concatenate([both[states:]] * tiles, axis=1)
            new = jnp.exp(now * decay) * hidden[r] + gain * push
            scan_buf[r, t : t + 1] = jnp.sum(read * new, axis=0, keepdims=True)
            state.append(new)
        hidden = tuple(state)
    for r in range(2):
        z = z_ref[r].astype(jnp.float32)
        full = scan_buf[r] + gain_ref[...] * sig_ref[r]
        out_ref[r] = (full * (z * jax.nn.sigmoid(z))).astype(out_ref.dtype)


def scan_call(reading, bc, signal, dt, z, bias, alog, gain, s0, s1):
    _, new_len, channels = signal.shape
    states, cols = alog.shape[0], bc.shape[2]
    chunk = CHUNK
    row = pl.BlockSpec((1, chunk), lambda i, s: (0, i))
    state = pl.BlockSpec((states, chunk), lambda i, s: (0, i))
    seq = pl.BlockSpec((None, 2, new_len, chunk), lambda i, s: (0, 0, 0, i))
    return pl.pallas_call(
        scan_kernel,
        grid_spec=pltpu.PrefetchScalarGridSpec(
            num_scalar_prefetch=1,
            grid=(channels // chunk,),
            in_specs=[
                pl.BlockSpec((2, new_len, cols), lambda i, s: (0, 0, 0)),
                pl.BlockSpec((2, new_len, chunk), lambda i, s: (0, 0, i)),
                seq,
                seq,
                row,
                state,
                row,
                state,
                state,
            ],
            out_specs=pl.BlockSpec((None, 2, new_len, chunk), lambda i, s: (0, 0, 0, i)),
            scratch_shapes=[
                pltpu.VMEM((2, new_len, cols, HD), jnp.float32),
                pltpu.VMEM((2, new_len, chunk), jnp.float32),
                pltpu.VMEM((2, new_len, chunk), jnp.float32),
                pltpu.VMEM((2, new_len, chunk), jnp.float32),
            ],
        ),
        out_shape=jax.ShapeDtypeStruct((1, 2, new_len, channels), jnp.bfloat16),
        name="scan",
    )(reading, bc, signal, dt, z, bias, alog, gain, s0, s1)


def local(
    queries,
    new_kv,
    cached_lookup_pairs,
    prefix_ssm,
    prefix_conv,
    pool_kv,
    pool_ssm,
    pool_conv,
    owner_id,
    readers,
    restore_src,
    restore_blk,
    state_src,
    ctx_blocks,
    mamba_x,
    mamba_z,
    mamba_dt,
    dt_bias,
    a_log,
    bypass_gain,
    conv_w,
    conv_b,
    w_bc,
):
    block_len = pool_kv.shape[2]
    own_index = lax.axis_index("replica")
    shared_kv, shared_ssm, shared_conv = (
        from_root(cached_lookup_pairs, "replica", owner_id[0]),
        from_root(prefix_ssm, "replica", owner_id[0]),
        from_root(prefix_conv, "replica", owner_id[0]),
    )
    my_sources = lax.dynamic_index_in_dim(restore_src, own_index, 0, keepdims=False)
    my_holder = lax.dynamic_index_in_dim(state_src, own_index, 0, keepdims=False)
    matched = restore_src == own_index
    served = jnp.any(matched, axis=1)
    picked = jnp.sum(jnp.where(matched, restore_blk, 0), axis=1)
    send_kv = jnp.where(
        served[:, None, None], jnp.take(pool_kv[0], picked, axis=0), jnp.zeros((), pool_kv.dtype)
    )
    holder = (state_src == own_index)[:, None, None]
    send_ssm = jnp.where(holder, pool_ssm, jnp.zeros((), pool_ssm.dtype))
    send_conv = jnp.where(holder, pool_conv, jnp.zeros((), pool_conv.dtype))
    got_kv, got_ssm, got_conv = (
        lax.all_to_all(send_kv[:, None], "replica", split_axis=0, concat_axis=1, tiled=True),
        lax.all_to_all(send_ssm[:, None], "replica", split_axis=0, concat_axis=1, tiled=True),
        lax.all_to_all(send_conv[:, None], "replica", split_axis=0, concat_axis=1, tiled=True),
    )
    restored_ssm = lax.dynamic_index_in_dim(got_ssm[0], my_holder, 0, keepdims=False)
    restored_conv = lax.dynamic_index_in_dim(got_conv[0], my_holder, 0, keepdims=False)
    reading = (readers > 0).astype(jnp.int32)
    signal, partial_bc = signal_call(
        reading, mamba_x, shared_conv[0], restored_conv, conv_w, conv_b[None], w_bc
    )
    state_bc = lax.psum(partial_bc, "channel")
    mamba_out = scan_call(
        reading, state_bc, signal, mamba_dt, mamba_z, dt_bias[None], a_log, bypass_gain[None],
        shared_ssm[0], restored_ssm
    )
    prefix = shared_kv[0]
    parts = prefix.shape[0] // block_len
    prefix_blocks = prefix.reshape(parts, prefix.shape[0] // parts, prefix.shape[1])
    fresh_out = attend(
        0, queries, prefix_blocks, lax.iota(jnp.int32, parts), reading * prefix.shape[0], new_kv
    )
    resumed_out = attend(1, queries, got_kv[0], my_sources, ctx_blocks * block_len, new_kv)
    return (jnp.stack([fresh_out, resumed_out])[None], mamba_out)


def placed_specs():
    return (
        P(("groups", "replica"), None, None, "channel"),
        P(("groups", "replica"), None, None, "channel"),
        P(("groups", "replica"), None, "channel"),
        P(("groups", "replica"), None, "channel"),
        P(("groups", "replica"), None, "channel"),
        P(("groups", "replica"), None, None, "channel"),
        P(("groups", "replica"), None, "channel"),
        P(("groups", "replica"), None, "channel"),
        P("groups"),
        P(("groups", "replica")),
        P("groups", None),
        P("groups", None),
        P("groups"),
        P(("groups", "replica")),
        P(("groups", "replica"), None, None, "channel"),
        P(("groups", "replica"), None, None, "channel"),
        P(("groups", "replica"), None, None, "channel"),
        P("channel"),
        P(None, "channel"),
        P("channel"),
        P(None, "channel"),
        P("channel"),
        P("channel", None),
    )


def solution(mesh):
    return jax.shard_map(
        local,
        mesh=mesh,
        in_specs=placed_specs(),
        out_specs=(
            P(("groups", "replica"), None, None, "channel"),
            P(("groups", "replica"), None, None, "channel"),
        ),
        check_vma=False,
    )
```

profile of v0, /device:TPU:0, one launch (start us, length us, event | category | flops | bytes accessed | tf_op | source)
XLA Modules:
  0.0 198.9 jit_solution(12907866967471605963)
XLA Ops:
  7.2 0.0 copy-start
  7.2 0.0 copy-start.5
  7.2 0.0 copy-start.6
  7.2 0.7 broadcast_compare_fusion.1
  7.9 1.6 broadcast_select_fusion.2
  9.6 7.3 %all-to-all-start.1 = ((bf16[8,1,3,4096]{3,2,1,0:T(4,128)(2,1)}), bf16[8,1,3,4096]{3,2,1,0:T(4,128)(2,1)S(1)}, u32[]{:S(2)}, u32[]{:S(2)}) async-start(bf16[8,1,3,4096]{3,2,1,0:T(4,128)(2,1)} %broadcast_select_fusion.2), calls=%async_computation.1 | async-start | bytes 524288 | tf_op jit(solution)/shard_map/all_to_all | solution.py:289
  16.9 2.0 %broadcast_select_fusion = bf16[8,1,16,4096]{3,2,1,0:T(8,128)(2,1)} fusion(pred[8]{0:T(512)(128)(4,1)S(1)} %broadcast_compare_fusion.1, bf16[16,4096]{1,0:T(8,128)(2,1)} %bitcast.39), kind=kLoop, calls=%fused_computation.3 | loop fusion | flops 524288 | bytes 1179656 | tf_op jit(solution)/shard_map/jit(_where)/select_n | solution.py:284
  18.9 6.9 %all-to-all-done.1 = bf16[8,1,3,4096]{3,2,1,0:T(4,128)(2,1)S(1)} async-done(((bf16[8,1,3,4096]{3,2,1,0:T(4,128)(2,1)}), bf16[8,1,3,4096]{3,2,1,0:T(4,128)(2,1)S(1)}, u32[]{:S(2)}, u32[]{:S(2)}) %all-to-all-start.1) | async-done | bytes 196640 | tf_op jit(solution)/shard_map/all_to_all | solution.py:289
  25.8 4.2 %all-to-all-start.2 = ((bf16[8,1,16,4096]{3,2,1,0:T(8,128)(2,1)}), bf16[8,1,16,4096]{3,2,1,0:T(8,128)(2,1)}, u32[]{:S(2)}, u32[]{:S(2)}) async-start(bf16[8,1,16,4096]{3,2,1,0:T(8,128)(2,1)} %broadcast_select_fusion), calls=%async_computation.2 | async-start | bytes 2097152 | tf_op jit(solution)/shard_map/all_to_all | solution.py:288
  30.0 0.0 copy-done.5
  30.1 0.0 copy-done.6
  30.1 0.0 copy-done
  30.1 0.7 gather_fusion
  30.8 1.6 fusion
  32.5 22.7 %all-to-all-done.2 = bf16[8,1,16,4096]{3,2,1,0:T(8,128)(2,1)} async-done(((bf16[8,1,16,4096]{3,2,1,0:T(8,128)(2,1)}), bf16[8,1,16,4096]{3,2,1,0:T(8,128)(2,1)}, u32[]{:S(2)}, u32[]{:S(2)}) %all-to-all-start.2) | async-done | bytes 1048608 | tf_op jit(solution)/shard_map/all_to_all | solution.py:288
  55.1 3.6 %all-to-all-start = ((bf16[8,1,256,512]{3,2,1,0:T(8,128)(2,1)}), bf16[8,1,256,512]{3,2,1,0:T(8,128)(2,1)S(1)}, u32[]{:S(2)}, u32[]{:S(2)}) async-start(bf16[8,1,256,512]{3,2,1,0:T(8,128)(2,1)} %fusion), calls=%async_computation | async-start | bytes 4194304 | tf_op jit(solution)/shard_map/all_to_all | solution.py:287
  58.7 0.0 copy-start.3
  58.8 0.0 copy-start.7
  58.8 0.0 all-reduce.3.cloned.1.call-start
  59.5 1.1 broadcast_select_fusion.1
  60.5 0.0 copy-done.3
  60.5 0.7 select_bitcast_fusion
  61.2 0.0 copy-start.4
  61.2 0.0 all-reduce.3.cloned.1.call-update
  61.2 0.8 dynamic-slice_reduce_fusion.refs_0_
  62.0 0.0 copy-done.7
  62.0 0.6 dynamic_slice.13
  65.2 2.3 %copy.26.wbc_ref = bf16[4096,32]{1,0:T(8,128)(2,1)} copy(bf16[4096,32]{0,1:T(8,128)(2,1)} %param.45) | data formatting | bytes 524288 | tf_op args[22]
  68.1 0.0 copy-done.4
  68.2 76.4 %psum.29.conv0_ref = bf16[3,4096]{1,0:T(4,128)(2,1)} all-reduce(bf16[3,4096]{1,0:T(4,128)(2,1)S(1)} %select_bitcast_fusion.1), channel_id=1, replica_groups=mesh['groups'=2,'replica'=8,'channel'=2] {'replica'}, use_global_device_ids=true, to_apply=%region_3.4 | all-reduce | flops 12288 | bytes 49152 | tf_op jit(solution)/shard_map/psum | solution.py:15
  144.6 0.6 dynamic-slice_bitcast_fusion.1.conv1_ref
  145.2 6.3 %signal.1 = (f32[2,32,4096]{2,1,0:T(8,128)}, f32[2,32,32]{2,1,0:T(8,128)}) custom-call(s32[1]{0:T(128)S(6)} %convert_element_type.9.read_ref, bf16[1,2,32,4096]{3,2,1,0:T(8,128)(2,1)} %x_ref.1, bf16[3,4096]{1,0:T(4,128)(2,1)} %psum.29.conv0_ref, bf16[3,4096]{1,0:T(4,128)(2,1)} %dynamic-slice_bitcast_fusion.1.conv1_ref, f32[4,4096]{1,0:T(4,128)} %w_ref.1, ...), custom_call_target="tpu_custom_call" | custom-call | tf_op jit(solution)/shard_map/signal/pallas_call | solution.py:136
  151.5 4.6 %psum.30.bc_ref = f32[2,32,32]{2,1,0:T(8,128)} all-reduce(f32[2,32,32]{2,1,0:T(8,128)} %get-tuple-element.4), channel_id=1, replica_groups=mesh['groups'=2,'replica'=8,'channel'=2] {'channel'}, use_global_device_ids=true, to_apply=%region_4.5 | all-reduce | flops 2048 | bytes 16384 | tf_op jit(solution)/shard_map/psum | solution.py:297
  156.1 13.4 %all-reduce.3.cloned.1.call-done = (bf16[4,256,512]{2,1,0:T(8,128)(2,1)}, bf16[16,4096]{1,0:T(8,128)(2,1)}) async-done(((bf16[4,256,512]{2,1,0:T(8,128)(2,1)}, bf16[16,4096]{1,0:T(8,128)(2,1)}), (bf16[4,256,512]{2,1,0:T(8,128)(2,1)}, bf16[16,4096]{1,0:T(8,128)(2,1)})) %all-reduce.3.cloned.1.call-update) | async-done | bytes 1179664 | tf_op jit(solution)/shard_map/psum | solution.py:15
  169.5 0.5 iota.3.refs_0_
  170.0 3.8 %attend.2 = bf16[32,2048]{1,0:T(8,128)(2,1)} custom-call(s32[4]{0:T(128)} %iota.3.refs_0_, s32[1]{0:T(128)S(6)} %mul.6.refs_1_, bf16[1,2,32,2048]{3,2,1,0:T(8,128)(2,1)} %refs_2_.3, bf16[4,256,512]{2,1,0:T(8,128)(2,1)} %get-tuple-element.6.refs_3_.refs_4_.refs_5_.refs_6_, bf16[4,256,512]{2,1,0:T(8,128)(2,1)} %get-tuple-element.6.refs_3_.refs_4_.refs_5_.refs_6_, ...), custom_call_target="tpu_custom_call" | custom-call | tf_op jit(solution)/shard_map/attend/pallas_call | solution.py:90
  173.8 1.6 dynamic-slice_bitcast_fusion.s1_ref
  175.4 9.8 %scan.1 = bf16[1,2,32,4096]{3,2,1,0:T(8,128)(2,1)} custom-call(s32[1]{0:T(128)S(6)} %convert_element_type.9.read_ref, f32[2,32,32]{2,1,0:T(8,128)} %psum.30.bc_ref, f32[2,32,4096]{2,1,0:T(8,128)} %get-tuple-element.5.sig_ref, bf16[1,2,32,4096]{3,2,1,0:T(8,128)(2,1)} %dt_ref.1, bf16[1,2,32,4096]{3,2,1,0:T(8,128)(2,1)} %z_ref.1, f32[1,4096]{1,0:T(1,128)} %bitcast.42, ...), custom_call_target="tpu_custom_call" | custom-call | tf_op jit(solution)/shard_map/scan/pallas_call | solution.py:214
  185.2 0.0 all-to-all-done
  185.2 0.0 copy-start.1
  185.2 1.3 copy-done.1
  186.5 0.0 copy-start.2
  186.5 3.9 %attend.3 = bf16[32,2048]{1,0:T(8,128)(2,1)} custom-call(s32[4]{0:T(128)} %dynamic-slice_reduce_fusion.refs_0_, s32[1]{0:T(128)S(6)} %mul.7.refs_1_, bf16[1,2,32,2048]{3,2,1,0:T(8,128)(2,1)} %refs_2_.3, bf16[8,256,512]{2,1,0:T(8,128)(2,1)} %bitcast.32, bf16[8,256,512]{2,1,0:T(8,128)(2,1)} %bitcast.33, bf16[8,256,512]{2,1,0:T(8,128)(2,1)} %bitcast.34, ...), custom_call_target="tpu_custom_call" | custom-call | tf_op jit(solution)/shard_map/attend/pallas_call | solution.py:90
  190.5 0.0 copy-done.2
  190.5 1.6 maximum_bitcast_fusion
  (6 shorter events, 0.1 us)
Async XLA Ops:
  7.2 23.0 %copy-start = (bf16[1,4,256,512]{3,2,1,0:T(8,128)(2,1)S(1)}, bf16[1,4,256,512]{3,2,1,0:T(8,128)(2,1)}, u32[]{:S(2)}) copy-start(bf16[1,4,256,512]{3,2,1,0:T(8,128)(2,1)} %param.28) | copy-start | bytes 3145732
  7.2 22.9 %copy-start.5 = (s32[8,4]{0,1:T(4,128)S(1)}, s32[8,4]{0,1:T(4,128)}, u32[]{:S(2)}) copy-start(s32[8,4]{0,1:T(4,128)} %param.33) | copy-start | bytes 388
  7.2 22.9 %copy-start.6 = (s32[8,4]{0,1:T(4,128)S(1)}, s32[8,4]{0,1:T(4,128)}, u32[]{:S(2)}) copy-start(s32[8,4]{0,1:T(4,128)} %param.34) | copy-start | bytes 388
  9.6 16.2 %all-to-all-start.1 = ((bf16[8,1,3,4096]{3,2,1,0:T(4,128)(2,1)}), bf16[8,1,3,4096]{3,2,1,0:T(4,128)(2,1)S(1)}, u32[]{:S(2)}, u32[]{:S(2)}) async-start(bf16[8,1,3,4096]{3,2,1,0:T(4,128)(2,1)} %broadcast_select_fusion.2), calls=%async_computation.1 | async-start | bytes 524288 | tf_op jit(solution)/shard_map/all_to_all | solution.py:289
  25.8 29.3 %all-to-all-start.2 = ((bf16[8,1,16,4096]{3,2,1,0:T(8,128)(2,1)}), bf16[8,1,16,4096]{3,2,1,0:T(8,128)(2,1)}, u32[]{:S(2)}, u32[]{:S(2)}) async-start(bf16[8,1,16,4096]{3,2,1,0:T(8,128)(2,1)} %broadcast_select_fusion), calls=%async_computation.2 | async-start | bytes 2097152 | tf_op jit(solution)/shard_map/all_to_all | solution.py:288
  55.1 130.1 %all-to-all-start = ((bf16[8,1,256,512]{3,2,1,0:T(8,128)(2,1)}), bf16[8,1,256,512]{3,2,1,0:T(8,128)(2,1)S(1)}, u32[]{:S(2)}, u32[]{:S(2)}) async-start(bf16[8,1,256,512]{3,2,1,0:T(8,128)(2,1)} %fusion), calls=%async_computation | async-start | bytes 4194304 | tf_op jit(solution)/shard_map/all_to_all | solution.py:287
  58.7 1.8 copy-start.3
  58.8 3.2 %copy-start.7 = (s32[8]{0:T(128)S(1)}, s32[8]{0:T(128)}, u32[]{:S(2)}) copy-start(s32[8]{0:T(128)} %param.35) | copy-start | bytes 100
  58.8 110.8 %all-reduce.3.cloned.1.call-start = ((), (), s32[]{:S(2)}) async-start(), calls=%async_computation.3 | async-start | bytes 2359296 | tf_op jit(solution)/shard_map/psum | solution.py:15
  61.2 6.9 %copy-start.4 = (bf16[1,3,4096]{2,1,0:T(4,128)(2,1)S(1)}, bf16[1,3,4096]{2,1,0:T(4,128)(2,1)}, u32[]{:S(2)}) copy-start(bf16[1,3,4096]{2,1,0:T(4,128)(2,1)} %param.27) | copy-start | bytes 73732
  185.2 1.3 copy-start.1
  186.5 3.9 %copy-start.2 = (bf16[32,2048]{1,0:T(8,128)(2,1)S(1)}, bf16[32,2048]{1,0:T(8,128)(2,1)}, u32[]{:S(2)}) copy-start(bf16[32,2048]{1,0:T(8,128)(2,1)} %attend.2) | copy-start | bytes 393220
Sparse Core Ops, SparseCore 0:
  63.7 105.8 all-reduce.2
where the time goes:
time: 200 us; the launch traced here: 199 us
  blocking collectives  81 us (40%)
  waiting for transfers between devices  43 us (22%)
  Pallas kernels  23.8 us (12%)
  between operations  18.1 us (9%)
  starting transfers between devices  15.2 us (8%)
  other arithmetic  9.46 us (5%)
  local copies, waits for them, and re-layouts  8.38 us (4%)
    psum x1, blocking collectives, from_root(): return lax.psum(kept, axis)  76.4 us
    all_to_all x1, waiting for transfers between devices, local(): lax.all_to_all(send_ssm[:, None], 'replica', split_axis=0, concat_axis=1,...  22.7 us
    psum x1, waiting for transfers between devices, from_root(): return lax.psum(kept, axis)  13.4 us
    pallas_call x1, Pallas kernels, scan_call(): pl.pallas_call(scan_kernel, grid_spec=pltpu.PrefetchScalarGridSpec(num_sc...  9.8 us
    pallas_call x2, Pallas kernels, attend(): pl.pallas_call(lambda *refs: attend_kernel(parts, *refs), grid_spec=pltpu...  7.72 us
    all_to_all x1, starting transfers between devices, local(): lax.all_to_all(send_conv[:, None], 'replica', split_axis=0, concat_axis=1...  7.31 us
    all_to_all x1, waiting for transfers between devices, local(): lax.all_to_all(send_conv[:, None], 'replica', split_axis=0, concat_axis=1...  6.89 us
    pallas_call x1, Pallas kernels, signal_call(): pl.pallas_call(signal_kernel, grid_spec=pltpu.PrefetchScalarGridSpec(num_...  6.28 us
  transfers between devices with their start and end apart: 4, of which 3 were waited for; matrix products, arithmetic and copies ran while one was open for 6% of the time, Pallas kernels for 10%

commit v1 on v0

--- a/solution.py
+++ b/solution.py
@@ -8,11 +8,6 @@
 HD = 128
 Q_PER_KV = 8
 CHUNK = 512
-
-
-def from_root(value, axis, source):
-    kept = jnp.where(lax.axis_index(axis) == source, value, 0).astype(value.dtype)
-    return lax.psum(kept, axis)
 
 
 def attend_kernel(parts, src_ref, live_ref, q_ref, *refs):
@@ -104,14 +99,15 @@
     )(source, live, queries, *([blocks] * parts), new_kv)
 
 
-def signal_kernel(read_ref, x_ref, conv0_ref, conv1_ref, w_ref, b_ref, wbc_ref, sig_ref, bc_ref, pad):
+def signal_kernel(read_ref, x_ref, state_ref, w_ref, b_ref, wbc_ref, sig_ref, bc_ref, pad):
     taps = w_ref.shape[0]
     new_len = x_ref.shape[1]
     reading = read_ref[0] > 0
     base = 8 - (taps - 1)
-    first = jnp.where(reading, conv0_ref[...].astype(jnp.float32), 0.0)
-    pad[0, base:8] = first
-    pad[1, base:8] = conv1_ref[...].astype(jnp.float32)
+    both = state_ref[...].astype(jnp.float32)
+    start = wbc_ref.shape[1] // 2
+    pad[0, base:8] = jnp.where(reading, both[0, start : start + taps - 1], 0.0)
+    pad[1, base:8] = both[1, start : start + taps - 1]
 
     @pl.when(pl.program_id(0) == 0)
     def _():
@@ -129,7 +125,7 @@
         )
 
 
-def signal_call(reading, x, conv0, conv1, w, b, wbc):
+def signal_call(reading, x, states, w, b, wbc):
     _, _, new_len, channels = x.shape
     taps, cols = w.shape[0], wbc.shape[1]
     chunk = CHUNK
@@ -140,8 +136,7 @@
             grid=(channels // chunk,),
             in_specs=[
                 pl.BlockSpec((None, 2, new_len, chunk), lambda i, s: (0, 0, 0, i)),
-                pl.BlockSpec((taps - 1, chunk), lambda i, s: (0, i)),
-                pl.BlockSpec((taps - 1, chunk), lambda i, s: (0, i)),
+                pl.BlockSpec((2, states.shape[1], chunk), lambda i, s: (0, 0, i)),
                 pl.BlockSpec((taps, chunk), lambda i, s: (0, i)),
                 pl.BlockSpec((1, chunk), lambda i, s: (0, i)),
                 pl.BlockSpec((chunk, cols), lambda i, s: (i, 0)),
@@ -157,11 +152,11 @@
             jax.ShapeDtypeStruct((2, new_len, cols), jnp.float32),
         ],
         name="signal",
-    )(reading, x, conv0, conv1, w, b, wbc)
+    )(reading, x, states, w, b, wbc)
 
 
 def scan_kernel(
-    read_ref, bc_ref, sig_ref, dt_ref, z_ref, bias_ref, alog_ref, gain_ref, s0_ref, s1_ref,
+    read_ref, bc_ref, sig_ref, dt_ref, z_ref, bias_ref, alog_ref, gain_ref, state_ref,
     out_ref, spread, step_buf, push_buf, scan_buf
 ):
     states, chunk = alog_ref.shape
@@ -182,8 +177,8 @@
         step_buf[r] = step
         push_buf[r] = step * sig_ref[r]
     hidden = (
-        jnp.where(read_ref[0] > 0, s0_ref[...].astype(jnp.float32), 0.0),
-        s1_ref[...].astype(jnp.float32),
+        jnp.where(read_ref[0] > 0, state_ref[0, :states].astype(jnp.float32), 0.0),
+        state_ref[1, :states].astype(jnp.float32),
     )
     tiles = chunk // HD
     for t in range(new_len):
@@ -204,7 +199,7 @@
         out_ref[r] = (full * (z * jax.nn.sigmoid(z))).astype(out_ref.dtype)
 
 
-def scan_call(reading, bc, signal, dt, z, bias, alog, gain, s0, s1):
+def scan_call(reading, bc, signal, dt, z, bias, alog, gain, packed):
     _, new_len, channels = signal.shape
     states, cols = alog.shape[0], bc.shape[2]
     chunk = CHUNK
@@ -224,8 +219,7 @@
                 row,
                 state,
                 row,
-                state,
-                state,
+                pl.BlockSpec((2, packed.shape[1], chunk), lambda i, s: (0, 0, i)),
             ],
             out_specs=pl.BlockSpec((None, 2, new_len, chunk), lambda i, s: (0, 0, 0, i)),
             scratch_shapes=[
@@ -237,7 +231,133 @@
         ),
         out_shape=jax.ShapeDtypeStruct((1, 2, new_len, channels), jnp.bfloat16),
         name="scan",
-    )(reading, bc, signal, dt, z, bias, alog, gain, s0, s1)
+    )(reading, bc, signal, dt, z, bias, alog, gain, packed)
+
+
+def exchange_kernel(
+    n, early, owner_ref, holder_ref, prefix_ref, state_ref, send_ref, shared_ref, states_ref, got_ref,
+    state_cand, prefix_cand, state_send, prefix_send, sends, recvs, local_sems
+):
+    me = lax.axis_index("replica")
+    rows = prefix_ref.shape[0] // n
+    cols = state_ref.shape[2] // n
+    barrier = pltpu.get_barrier_semaphore()
+    for s in range(1, n):
+        pl.semaphore_signal(
+            barrier, inc=1, device_id={"replica": lax.rem(me + s, n)}, device_id_type=pl.DeviceIdType.MESH
+        )
+
+    def row_piece(k):
+        return pl.ds(pl.multiple_of(k * rows, rows), rows)
+
+    def col_piece(k):
+        return pl.ds(pl.multiple_of(k * cols, HD), cols)
+
+    def remote(kind, s, source, target):
+        return pltpu.make_async_remote_copy(
+            src_ref=source,
+            dst_ref=target,
+            send_sem=sends.at[kind, s],
+            recv_sem=recvs.at[kind, s],
+            device_id={"replica": lax.rem(me + s, n)},
+            device_id_type=pl.DeviceIdType.MESH,
+        )
+
+    own_state = pltpu.make_async_copy(
+        state_ref.at[:, :, col_piece(me)], state_cand.at[me], local_sems.at[0]
+    )
+    own_prefix = pltpu.make_async_copy(
+        prefix_ref.at[row_piece(me)], prefix_cand.at[me], local_sems.at[1]
+    )
+    own_block = pltpu.make_async_copy(send_ref.at[me], got_ref.at[me], local_sems.at[2])
+    own_state.start()
+    own_prefix.start()
+    own_block.start()
+    pl.semaphore_wait(barrier, n - 1)
+
+    first_state, first_prefix, blocks, second_state, second_prefix = [], [], [], [], []
+    for s in range(1, n):
+        peer = lax.rem(me + s, n)
+        copy = remote(0, s, state_ref.at[:, :, col_piece(peer)], state_cand.at[me])
+        copy.start()
+        first_state.append(copy)
+    for s in range(1, n):
+        peer = lax.rem(me + s, n)
+        copy = remote(1, s, prefix_ref.at[row_piece(peer)], prefix_cand.at[me])
+        copy.start()
+        first_prefix.append(copy)
+
+    def send_block(s):
+        peer = lax.rem(me + s, n)
+        copy = remote(2, s, send_ref.at[peer], got_ref.at[me])
+        copy.start()
+        blocks.append(copy)
+
+    own_state.wait()
+    for copy in first_state:
+        copy.wait()
+    owner = owner_ref[0]
+    for d in range(n):
+        state_send[d, 0] = state_cand[owner, 0]
+        state_send[d, 1] = state_cand[holder_ref[d], 1]
+    for s in range(1, early):
+        send_block(s)
+    for s in range(1, n):
+        peer = lax.rem(me + s, n)
+        copy = remote(3, s, state_send.at[peer], states_ref.at[:, :, col_piece(me)])
+        copy.start()
+        second_state.append(copy)
+    mine_state = pltpu.make_async_copy(
+        state_send.at[me], states_ref.at[:, :, col_piece(me)], local_sems.at[3]
+    )
+    mine_state.start()
+    own_prefix.wait()
+    for copy in first_prefix:
+        copy.wait()
+    prefix_send[...] = prefix_cand[owner]
+    for s in range(1, n):
+        copy = remote(4, s, prefix_send, shared_ref.at[row_piece(me)])
+        copy.start()
+        second_prefix.append(copy)
+    mine_prefix = pltpu.make_async_copy(prefix_send, shared_ref.at[row_piece(me)], local_sems.at[4])
+    mine_prefix.start()
+    for s in range(early, n):
+        send_block(s)
+    own_block.wait()
+    mine_state.wait()
+    mine_prefix.wait()
+    for copy in second_state + second_prefix + blocks:
+        copy.wait()
+
+
+def exchange(owner_id, state_src, prefix, states, send_kv):
+    n = send_kv.shape[0]
+    any_spec = pl.BlockSpec(memory_space=pl.ANY)
+    smem = pl.BlockSpec(memory_space=pltpu.SMEM)
+    rows, cols = prefix.shape[0] // n, states.shape[2] // n
+    two, height = states.shape[:2]
+    early = 1 + n // 4
+    return pl.pallas_call(
+        lambda *refs: exchange_kernel(n, early, *refs),
+        in_specs=[smem, smem, any_spec, any_spec, any_spec],
+        out_specs=[any_spec] * 3,
+        out_shape=[
+            jax.ShapeDtypeStruct(prefix.shape, prefix.dtype),
+            jax.ShapeDtypeStruct(states.shape, states.dtype),
+            jax.ShapeDtypeStruct(send_kv.shape, send_kv.dtype),
+        ],
+        scratch_shapes=[
+            pltpu.VMEM((n, two, height, cols), states.dtype),
+            pltpu.VMEM((n, rows, prefix.shape[1]), prefix.dtype),
+            pltpu.VMEM((n, two, height, cols), states.dtype),
+            pltpu.VMEM((rows, prefix.shape[1]), prefix.dtype),
+            pltpu.SemaphoreType.DMA((5, n)),
+            pltpu.SemaphoreType.DMA((5, n)),
+            pltpu.SemaphoreType.DMA((5,)),
+        ],
+        compiler_params=pltpu.CompilerParams(collective_id=0, has_side_effects=True),
+        name="exchange",
+    )(owner_id, state_src, prefix, states, send_kv)
 
 
 def local(
@@ -267,45 +387,30 @@
 ):
     block_len = pool_kv.shape[2]
     own_index = lax.axis_index("replica")
-    shared_kv, shared_ssm, shared_conv = (
-        from_root(cached_lookup_pairs, "replica", owner_id[0]),
-        from_root(prefix_ssm, "replica", owner_id[0]),
-        from_root(prefix_conv, "replica", owner_id[0]),
-    )
     my_sources = lax.dynamic_index_in_dim(restore_src, own_index, 0, keepdims=False)
-    my_holder = lax.dynamic_index_in_dim(state_src, own_index, 0, keepdims=False)
-    matched = restore_src == own_index
-    served = jnp.any(matched, axis=1)
-    picked = jnp.sum(jnp.where(matched, restore_blk, 0), axis=1)
-    send_kv = jnp.where(
-        served[:, None, None], jnp.take(pool_kv[0], picked, axis=0), jnp.zeros((), pool_kv.dtype)
-    )
-    holder = (state_src == own_index)[:, None, None]
-    send_ssm = jnp.where(holder, pool_ssm, jnp.zeros((), pool_ssm.dtype))
-    send_conv = jnp.where(holder, pool_conv, jnp.zeros((), pool_conv.dtype))
-    got_kv, got_ssm, got_conv = (
-        lax.all_to_all(send_kv[:, None], "replica", split_axis=0, concat_axis=1, tiled=True),
-        lax.all_to_all(send_ssm[:, None], "replica", split_axis=0, concat_axis=1, tiled=True),
-        lax.all_to_all(send_conv[:, None], "replica", split_axis=0, concat_axis=1, tiled=True),
-    )
-    restored_ssm = lax.dynamic_index_in_dim(got_ssm[0], my_holder, 0, keepdims=False)
-    restored_conv = lax.dynamic_index_in_dim(got_conv[0], my_holder, 0, keepdims=False)
+    picked = jnp.sum(jnp.where(restore_src == own_index, restore_blk, 0), axis=1)
+    send_kv = jnp.take(pool_kv[0], picked, axis=0, mode="clip")
+    state_dim, taps = prefix_ssm.shape[1], prefix_conv.shape[1]
+    pad = -(state_dim + taps) % 8
+    states = jnp.stack(
+        [
+            jnp.pad(jnp.concatenate([ssm[0], conv[0]], axis=0), ((0, pad), (0, 0)))
+            for ssm, conv in ((prefix_ssm, prefix_conv), (pool_ssm, pool_conv))
+        ]
+    )
+    prefix, states, got_kv = exchange(owner_id, state_src, cached_lookup_pairs[0], states, send_kv)
     reading = (readers > 0).astype(jnp.int32)
-    signal, partial_bc = signal_call(
-        reading, mamba_x, shared_conv[0], restored_conv, conv_w, conv_b[None], w_bc
-    )
+    signal, partial_bc = signal_call(reading, mamba_x, states, conv_w, conv_b[None], w_bc)
     state_bc = lax.psum(partial_bc, "channel")
     mamba_out = scan_call(
-        reading, state_bc, signal, mamba_dt, mamba_z, dt_bias[None], a_log, bypass_gain[None],
-        shared_ssm[0], restored_ssm
-    )
-    prefix = shared_kv[0]
+        reading, state_bc, signal, mamba_dt, mamba_z, dt_bias[None], a_log, bypass_gain[None], states
+    )
     parts = prefix.shape[0] // block_len
-    prefix_blocks = prefix.reshape(parts, prefix.shape[0] // parts, prefix.shape[1])
+    prefix_blocks = prefix.reshape(parts, block_len, prefix.shape[1])
     fresh_out = attend(
         0, queries, prefix_blocks, lax.iota(jnp.int32, parts), reading * prefix.shape[0], new_kv
     )
-    resumed_out = attend(1, queries, got_kv[0], my_sources, ctx_blocks * block_len, new_kv)
+    resumed_out = attend(1, queries, got_kv, my_sources, ctx_blocks * block_len, new_kv)
     return (jnp.stack([fresh_out, resumed_out])[None], mamba_out)
 
 

time: 200 us -> 154 us (0.77)
  the two profiles are of different devices: /device:TPU:0 before, /device:TPU:29 now
where the time goes in v1:
time: 154 us; the launch traced here: 153 us
  Pallas kernels  136 us (88%)
  blocking collectives  6.01 us (4%)
  local copies, waits for them, and re-layouts  4.97 us (3%)
  other arithmetic  3.27 us (2%)
  between operations  2.65 us (2%)
    pallas_call x1, Pallas kernels, exchange(): pl.pallas_call(lambda *refs: exchange_kernel(n, early, *refs), in_specs=[...  112 us
    pallas_call x1, Pallas kernels, scan_call(): pl.pallas_call(scan_kernel, grid_spec=pltpu.PrefetchScalarGridSpec(num_sc...  9.8 us
    pallas_call x2, Pallas kernels, attend(): pl.pallas_call(lambda *refs: attend_kernel(parts, *refs), grid_spec=pltpu...  7.71 us
    pallas_call x1, Pallas kernels, signal_call(): pl.pallas_call(signal_kernel, grid_spec=pltpu.PrefetchScalarGridSpec(num_...  6.33 us
    psum x1, blocking collectives, local(): state_bc = lax.psum(partial_bc, 'channel')  6.01 us

profile of v1, /device:TPU:29, one launch (start us, length us, event | category | flops | bytes accessed | tf_op | source)
XLA Modules:
  0.0 153.1 jit_solution(17007503588060369043)
XLA Ops:
  0.6 0.0 copy-start
  0.6 0.8 select_reduce_fusion
  1.5 0.4 copy-done
  1.9 0.0 copy-start.3
  1.9 0.0 copy-start.4
  1.9 0.0 copy-start.5
  1.9 0.0 copy-start.6
  1.9 2.0 %gather_fusion = bf16[8,256,512]{2,1,0:T(8,128)(2,1)} fusion(bf16[4,256,512]{2,1,0:T(8,128)(2,1)S(1)} %bitcast.18, s32[1024]{0:T(1024)S(1)} %pad_clamp_fusion), kind=kCustom, calls=%fused_computation | custom fusion | bytes 4194336 | tf_op jit(solution)/shard_map/jit(_take)/gather | solution.py:392
  3.9 0.0 copy-done.3
  3.9 0.0 copy-done.4
  3.9 0.0 copy-done.5
  3.9 0.0 copy-done.6
  4.0 0.0 copy-start.2
  4.0 0.8 pad_maximum_fusion.refs_3_
  5.4 112.3 %exchange.1 = (bf16[1024,512]{1,0:T(8,128)(2,1)}, bf16[2,24,4096]{2,1,0:T(8,128)(2,1)}, bf16[8,256,512]{2,1,0:T(8,128)(2,1)}) custom-call(s32[1]{0:T(128)S(6)} %copy.26.refs_0_, s32[8]{0:T(128)} %refs_1_.1, bf16[1024,512]{1,0:T(8,128)(2,1)} %bitcast.23, bf16[2,24,4096]{2,1,0:T(8,128)(2,1)} %pad_maximum_fusion.refs_3_, bf16[8,256,512]{2,1,0:T(8,128)(2,1)} %gather_fusion), custom_call_target="tpu_custom_call" | custom-call | tf_op jit(solution)/shard_map/exchange/pallas_call | solution.py:340
  118.4 0.0 copy-done.2
  118.4 1.3 copy.25.wbc_ref
  119.7 6.3 %signal.1 = (f32[2,32,4096]{2,1,0:T(8,128)}, f32[2,32,32]{2,1,0:T(8,128)}) custom-call(s32[1]{0:T(128)S(6)} %convert_element_type.6.read_ref, bf16[1,2,32,4096]{3,2,1,0:T(8,128)(2,1)} %x_ref.1, bf16[2,24,4096]{2,1,0:T(8,128)(2,1)} %get-tuple-element.9.state_ref, f32[4,4096]{1,0:T(4,128)} %w_ref.1, f32[1,4096]{1,0:T(1,128)} %bitcast.30, ...), custom_call_target="tpu_custom_call" | custom-call | tf_op jit(solution)/shard_map/signal/pallas_call | solution.py:132
  126.0 0.0 copy-start.7
  126.0 6.0 %psum.7.bc_ref = f32[2,32,32]{2,1,0:T(8,128)} all-reduce(f32[2,32,32]{2,1,0:T(8,128)} %get-tuple-element.10), channel_id=1, replica_groups=mesh['groups'=2,'replica'=8,'channel'=2] {'channel'}, use_global_device_ids=true, to_apply=%region_1.2 | all-reduce | flops 2048 | bytes 16384 | tf_op jit(solution)/shard_map/psum | solution.py:404
  132.1 9.8 %scan.1 = bf16[1,2,32,4096]{3,2,1,0:T(8,128)(2,1)} custom-call(s32[1]{0:T(128)S(6)} %convert_element_type.6.read_ref, f32[2,32,32]{2,1,0:T(8,128)} %psum.7.bc_ref, f32[2,32,4096]{2,1,0:T(8,128)} %get-tuple-element.11.sig_ref, bf16[1,2,32,4096]{3,2,1,0:T(8,128)(2,1)} %dt_ref.1, bf16[1,2,32,4096]{3,2,1,0:T(8,128)(2,1)} %z_ref.1, f32[1,4096]{1,0:T(1,128)} %bitcast.31, ...), custom_call_target="tpu_custom_call" | custom-call | tf_op jit(solution)/shard_map/scan/pallas_call | solution.py:209
  141.9 0.0 copy-done.7
  141.9 0.7 dynamic-slice_reduce_fusion.refs_0_
  143.2 3.8 %attend.3 = bf16[32,2048]{1,0:T(8,128)(2,1)} custom-call(s32[4]{0:T(128)} %dynamic-slice_reduce_fusion.refs_0_, s32[1]{0:T(128)S(6)} %mul.7.refs_1_, bf16[1,2,32,2048]{3,2,1,0:T(8,128)(2,1)} %refs_2_.3, bf16[8,256,512]{2,1,0:T(8,128)(2,1)} %get-tuple-element.8.refs_3_.refs_4_.refs_5_.refs_6_, ...), custom_call_target="tpu_custom_call" | custom-call | tf_op jit(solution)/shard_map/attend/pallas_call | solution.py:85
  147.0 0.5 iota.3.refs_0_
  147.5 0.0 copy-start.1
  147.5 3.9 %attend.2 = bf16[32,2048]{1,0:T(8,128)(2,1)} custom-call(s32[4]{0:T(128)} %iota.3.refs_0_, s32[1]{0:T(128)S(6)} %mul.6.refs_1_, bf16[1,2,32,2048]{3,2,1,0:T(8,128)(2,1)} %refs_2_.3, bf16[4,256,512]{2,1,0:T(8,128)(2,1)} %bitcast.19, bf16[4,256,512]{2,1,0:T(8,128)(2,1)} %bitcast.20, bf16[4,256,512]{2,1,0:T(8,128)(2,1)} %bitcast.21, ...), custom_call_target="tpu_custom_call" | custom-call | tf_op jit(solution)/shard_map/attend/pallas_call | solution.py:85
  151.4 0.0 copy-done.1
  151.4 1.6 %maximum_bitcast_fusion = bf16[1,2,32,2048]{3,2,1,0:T(8,128)(2,1)} fusion(bf16[1,32,2048]{2,1,0:T(8,128)(2,1)S(1)} %bitcast.24, bf16[1,32,2048]{2,1,0:T(8,128)(2,1)} %bitcast.25), kind=kLoop, calls=%fused_computation.7 | loop fusion | flops 131072 | bytes 524288 | tf_op jit(solution)/shard_map/broadcast_in_dim | solution.py:414
  (2 shorter events, 0.1 us)
Async XLA Ops:
  0.6 1.3 copy-start
  1.9 2.0 %copy-start.3 = (bf16[1,16,4096]{2,1,0:T(8,128)(2,1)S(1)}, bf16[1,16,4096]{2,1,0:T(8,128)(2,1)}, u32[]{:S(2)}) copy-start(bf16[1,16,4096]{2,1,0:T(8,128)(2,1)} %param.26) | copy-start | bytes 393220
  1.9 2.0 %copy-start.4 = (bf16[1,16,4096]{2,1,0:T(8,128)(2,1)S(1)}, bf16[1,16,4096]{2,1,0:T(8,128)(2,1)}, u32[]{:S(2)}) copy-start(bf16[1,16,4096]{2,1,0:T(8,128)(2,1)} %param.29) | copy-start | bytes 393220
  1.9 2.0 %copy-start.5 = (bf16[1,3,4096]{2,1,0:T(4,128)(2,1)S(1)}, bf16[1,3,4096]{2,1,0:T(4,128)(2,1)}, u32[]{:S(2)}) copy-start(bf16[1,3,4096]{2,1,0:T(4,128)(2,1)} %param.27) | copy-start | bytes 73732
  1.9 2.0 %copy-start.6 = (bf16[1,3,4096]{2,1,0:T(4,128)(2,1)S(1)}, bf16[1,3,4096]{2,1,0:T(4,128)(2,1)}, u32[]{:S(2)}) copy-start(bf16[1,3,4096]{2,1,0:T(4,128)(2,1)} %param.30) | copy-start | bytes 73732
  4.0 114.4 %copy-start.2 = (bf16[4096,32]{0,1:T(8,128)(2,1)S(1)}, bf16[4096,32]{0,1:T(8,128)(2,1)}, u32[]{:S(2)}) copy-start(bf16[4096,32]{0,1:T(8,128)(2,1)} %param.45) | copy-start | bytes 786436
  126.0 15.8 %copy-start.7 = (s32[8,4]{0,1:T(4,128)S(1)}, s32[8,4]{0,1:T(4,128)}, u32[]{:S(2)}) copy-start(s32[8,4]{0,1:T(4,128)} %param.33) | copy-start | bytes 388
  147.5 3.9 %copy-start.1 = (bf16[32,2048]{1,0:T(8,128)(2,1)S(1)}, bf16[32,2048]{1,0:T(8,128)(2,1)}, u32[]{:S(2)}) copy-start(bf16[32,2048]{1,0:T(8,128)(2,1)} %attend.3) | copy-start | bytes 393220

commit v2 on v1

--- a/solution.py
+++ b/solution.py
@@ -7,7 +7,7 @@
 
 HD = 128
 Q_PER_KV = 8
-CHUNK = 512
+CHUNKS = 4
 
 
 def attend_kernel(parts, src_ref, live_ref, q_ref, *refs):
@@ -33,13 +33,13 @@
         for ref in ctx_refs:
             piece = (
                 lax.dot_general(
-                    query, ref[0, :, key_cols], contract, preferred_element_type=jnp.float32
+                    query, ref[:, key_cols], contract, preferred_element_type=jnp.float32
                 )
                 * factor
             )
             position = start + lax.broadcasted_iota(jnp.int32, piece.shape, 1)
             scores.append(jnp.where(position < live, piece, -jnp.inf))
-            start += ref.shape[1]
+            start += ref.shape[0]
         fresh = (
             lax.dot_general(
                 query, new_ref[:, key_cols], contract, preferred_element_type=jnp.float32
@@ -65,7 +65,7 @@
             total = total + jnp.sum(weight, axis=1, keepdims=True)
             mixed = mixed + jnp.dot(
                 weight.astype(jnp.bfloat16),
-                ref[0, :, value_cols],
+                ref[:, value_cols],
                 preferred_element_type=jnp.float32,
             )
         result = (mixed / total).astype(out_ref.dtype)
@@ -74,13 +74,13 @@
             out_ref[:, at : at + HD] = result[g * new_len : (g + 1) * new_len]
 
 
-def attend(request, queries, blocks, source, live, new_kv):
+def attend(request, queries, blocks, block_len, source, live, new_kv):
     parts = source.shape[0]
-    _, block_len, width = blocks.shape
+    width = blocks.shape[1]
     _, _, new_len, q_width = queries.shape
 
     def pick(j):
-        return pl.BlockSpec((1, block_len, width), lambda i, s, l: (s[j], 0, 0))
+        return pl.BlockSpec((block_len, width), lambda i, s, l: (s[j], 0))
 
     return pl.pallas_call(
         lambda *refs: attend_kernel(parts, *refs),
@@ -99,15 +99,15 @@
     )(source, live, queries, *([blocks] * parts), new_kv)
 
 
-def signal_kernel(read_ref, x_ref, state_ref, w_ref, b_ref, wbc_ref, sig_ref, bc_ref, pad):
+def signal_kernel(read_ref, x_ref, shared_ref, pool_ref, w_ref, b_ref, wbc_ref, sig_ref, bc_ref, pad):
     taps = w_ref.shape[0]
     new_len = x_ref.shape[1]
     reading = read_ref[0] > 0
     base = 8 - (taps - 1)
-    both = state_ref[...].astype(jnp.float32)
     start = wbc_ref.shape[1] // 2
-    pad[0, base:8] = jnp.where(reading, both[0, start : start + taps - 1], 0.0)
-    pad[1, base:8] = both[1, start : start + taps - 1]
+    shared = shared_ref[...].astype(jnp.float32)[start : start + taps - 1]
+    pad[0, base:8] = jnp.where(reading, shared, 0.0)
+    pad[1, base:8] = pool_ref[...].astype(jnp.float32)[start : start + taps - 1]
 
     @pl.when(pl.program_id(0) == 0)
     def _():
@@ -125,10 +125,10 @@
         )
 
 
-def signal_call(reading, x, states, w, b, wbc):
+def signal_call(reading, x, shared, offset, pool, w, b, wbc):
     _, _, new_len, channels = x.shape
     taps, cols = w.shape[0], wbc.shape[1]
-    chunk = CHUNK
+    chunk = pool.shape[2]
     return pl.pallas_call(
         signal_kernel,
         grid_spec=pltpu.PrefetchScalarGridSpec(
@@ -136,7 +136,8 @@
             grid=(channels // chunk,),
             in_specs=[
                 pl.BlockSpec((None, 2, new_len, chunk), lambda i, s: (0, 0, 0, i)),
-                pl.BlockSpec((2, states.shape[1], chunk), lambda i, s: (0, 0, i)),
+                pl.BlockSpec((None, shared.shape[1], chunk), lambda i, s: (offset + i, 0, 0)),
+                pl.BlockSpec((None, pool.shape[1], chunk), lambda i, s: (i, 0, 0)),
                 pl.BlockSpec((taps, chunk), lambda i, s: (0, i)),
                 pl.BlockSpec((1, chunk), lambda i, s: (0, i)),
                 pl.BlockSpec((chunk, cols), lambda i, s: (i, 0)),
@@ -152,11 +153,11 @@
             jax.ShapeDtypeStruct((2, new_len, cols), jnp.float32),
         ],
         name="signal",
-    )(reading, x, states, w, b, wbc)
+    )(reading, x, shared, pool, w, b, wbc)
 
 
 def scan_kernel(
-    read_ref, bc_ref, sig_ref, dt_ref, z_ref, bias_ref, alog_ref, gain_ref, state_ref,
+    read_ref, bc_ref, sig_ref, dt_ref, z_ref, bias_ref, alog_ref, gain_ref, shared_ref, pool_ref,
     out_ref, spread, step_buf, push_buf, scan_buf
 ):
     states, chunk = alog_ref.shape
@@ -177,8 +178,8 @@
         step_buf[r] = step
         push_buf[r] = step * sig_ref[r]
     hidden = (
-        jnp.where(read_ref[0] > 0, state_ref[0, :states].astype(jnp.float32), 0.0),
-        state_ref[1, :states].astype(jnp.float32),
+        jnp.where(read_ref[0] > 0, shared_ref[...].astype(jnp.float32)[:states], 0.0),
+        pool_ref[...].astype(jnp.float32)[:states],
     )
     tiles = chunk // HD
     for t in range(new_len):
@@ -199,10 +200,10 @@
         out_ref[r] = (full * (z * jax.nn.sigmoid(z))).astype(out_ref.dtype)
 
 
-def scan_call(reading, bc, signal, dt, z, bias, alog, gain, packed):
+def scan_call(reading, bc, signal, dt, z, bias, alog, gain, shared, offset, pool):
     _, new_len, channels = signal.shape
     states, cols = alog.shape[0], bc.shape[2]
-    chunk = CHUNK
+    chunk = pool.shape[2]
     row = pl.BlockSpec((1, chunk), lambda i, s: (0, i))
     state = pl.BlockSpec((states, chunk), lambda i, s: (0, i))
     seq = pl.BlockSpec((None, 2, new_len, chunk), lambda i, s: (0, 0, 0, i))
@@ -219,7 +220,8 @@
                 row,
                 state,
                 row,
-                pl.BlockSpec((2, packed.shape[1], chunk), lambda i, s: (0, 0, i)),
+                pl.BlockSpec((None, shared.shape[1], chunk), lambda i, s: (offset + i, 0, 0)),
+                pl.BlockSpec((None, pool.shape[1], chunk), lambda i, s: (i, 0, 0)),
             ],
             out_specs=pl.BlockSpec((None, 2, new_len, chunk), lambda i, s: (0, 0, 0, i)),
             scratch_shapes=[
@@ -231,102 +233,165 @@
         ),
         out_shape=jax.ShapeDtypeStruct((1, 2, new_len, channels), jnp.bfloat16),
         name="scan",
-    )(reading, bc, signal, dt, z, bias, alog, gain, packed)
+    )(reading, bc, signal, dt, z, bias, alog, gain, shared, pool)
 
 
 def exchange_kernel(
-    n, early, owner_ref, holder_ref, prefix_ref, state_ref, send_ref, shared_ref, states_ref, got_ref,
-    state_cand, prefix_cand, state_send, prefix_send, sends, recvs, local_sems
+    n, owner_ref, holder_ref, prefix_ref, state_ref, send_ref, shared_ref, states_ref, got_ref,
+    state_cand, state_send, own, side, rightward, leftward, to_right, to_left, final,
+    sends, recvs, chain_sends, chain_recvs, local_sems
 ):
     me = lax.axis_index("replica")
-    rows = prefix_ref.shape[0] // n
-    cols = state_ref.shape[2] // n
+    chunks = prefix_ref.shape[1]
+    line, half = me // 2, lax.rem(me, 2)
+    length = n // 2
+    last = length - 1
+    partner = line * 2 + 1 - half
+    owner = owner_ref[0]
+    owner_line = owner // 2
     barrier = pltpu.get_barrier_semaphore()
     for s in range(1, n):
         pl.semaphore_signal(
             barrier, inc=1, device_id={"replica": lax.rem(me + s, n)}, device_id_type=pl.DeviceIdType.MESH
         )
 
-    def row_piece(k):
-        return pl.ds(pl.multiple_of(k * rows, rows), rows)
-
-    def col_piece(k):
-        return pl.ds(pl.multiple_of(k * cols, HD), cols)
-
-    def remote(kind, s, source, target):
+    def remote(source, target, send_sem, recv_sem, peer):
         return pltpu.make_async_remote_copy(
             src_ref=source,
             dst_ref=target,
-            send_sem=sends.at[kind, s],
-            recv_sem=recvs.at[kind, s],
-            device_id={"replica": lax.rem(me + s, n)},
+            send_sem=send_sem,
+            recv_sem=recv_sem,
+            device_id={"replica": peer},
             device_id_type=pl.DeviceIdType.MESH,
         )
 
-    own_state = pltpu.make_async_copy(
-        state_ref.at[:, :, col_piece(me)], state_cand.at[me], local_sems.at[0]
-    )
-    own_prefix = pltpu.make_async_copy(
-        prefix_ref.at[row_piece(me)], prefix_cand.at[me], local_sems.at[1]
-    )
+    def spread(kind, s, source, target):
+        return remote(
+            source, target, sends.at[kind, s], recvs.at[kind, s], lax.rem(me + s, n)
+        )
+
+    def chain(kind, c, source, target, peer):
+        return remote(source, target, chain_sends.at[kind, c], chain_recvs.at[kind, c], peer)
+
+    own_prefix = pltpu.make_async_copy(prefix_ref.at[half], own, local_sems.at[0])
+    own_state = pltpu.make_async_copy(state_ref.at[me], state_cand.at[me], local_sems.at[1])
     own_block = pltpu.make_async_copy(send_ref.at[me], got_ref.at[me], local_sems.at[2])
+    own_prefix.start()
     own_state.start()
-    own_prefix.start()
     own_block.start()
     pl.semaphore_wait(barrier, n - 1)
 
-    first_state, first_prefix, blocks, second_state, second_prefix = [], [], [], [], []
+    first_state, blocks, second_state, sideways = [], [], [], []
     for s in range(1, n):
-        peer = lax.rem(me + s, n)
-        copy = remote(0, s, state_ref.at[:, :, col_piece(peer)], state_cand.at[me])
+        copy = spread(0, s, state_ref.at[lax.rem(me + s, n)], state_cand.at[me])
         copy.start()
         first_state.append(copy)
-    for s in range(1, n):
-        peer = lax.rem(me + s, n)
-        copy = remote(1, s, prefix_ref.at[row_piece(peer)], prefix_cand.at[me])
+    for c in range(chunks):
+        copy = chain(0, c, prefix_ref.at[1 - half, c], side.at[c], partner)
         copy.start()
-        first_prefix.append(copy)
+        sideways.append(copy)
 
     def send_block(s):
-        peer = lax.rem(me + s, n)
-        copy = remote(2, s, send_ref.at[peer], got_ref.at[me])
+        copy = spread(1, s, send_ref.at[lax.rem(me + s, n)], got_ref.at[me])
         copy.start()
         blocks.append(copy)
 
+    send_block(1)
     own_state.wait()
     for copy in first_state:
         copy.wait()
-    owner = owner_ref[0]
     for d in range(n):
-        state_send[d, 0] = state_cand[owner, 0]
-        state_send[d, 1] = state_cand[holder_ref[d], 1]
-    for s in range(1, early):
-        send_block(s)
+        state_send[d] = state_cand[holder_ref[d]]
     for s in range(1, n):
-        peer = lax.rem(me + s, n)
-        copy = remote(3, s, state_send.at[peer], states_ref.at[:, :, col_piece(me)])
+        copy = spread(2, s, state_send.at[lax.rem(me + s, n)], states_ref.at[me])
         copy.start()
         second_state.append(copy)
-    mine_state = pltpu.make_async_copy(
-        state_send.at[me], states_ref.at[:, :, col_piece(me)], local_sems.at[3]
-    )
+    mine_state = pltpu.make_async_copy(state_send.at[me], states_ref.at[me], local_sems.at[3])
     mine_state.start()
     own_prefix.wait()
-    for copy in first_prefix:
-        copy.wait()
-    prefix_send[...] = prefix_cand[owner]
-    for s in range(1, n):
-        copy = remote(4, s, prefix_send, shared_ref.at[row_piece(me)])
-        copy.start()
-        second_prefix.append(copy)
-    mine_prefix = pltpu.make_async_copy(prefix_send, shared_ref.at[row_piece(me)], local_sems.at[4])
-    mine_prefix.start()
-    for s in range(early, n):
+
+    def right_copy(c):
+        return chain(1, c, to_right.at[c], rightward.at[c], lax.rem(me + 2, n))
+
+    def left_copy(c):
+        return chain(2, c, to_left.at[c], leftward.at[c], lax.rem(me + n - 2, n))
+
+    def final_copy(c):
+        return chain(3, c, final.at[c], shared_ref.at[half, c], partner)
+
+    def keep_copy(c):
+        return pltpu.make_async_copy(final.at[c], shared_ref.at[half, c], local_sems.at[4 + c])
+
+    def here(c):
+        return jnp.where(owner == me, own[c], side[c])
+
+    near, far = jnp.minimum(line, last - line), jnp.maximum(line, last - line)
+    steps = chunks + length - 1
+    sent = 2
+    for t in range(steps):
+        c_near, c_right, c_left, c_far = t - near, t - line, t - (last - line), t - far
+
+        @pl.when((c_near >= 0) & (c_near < chunks))
+        def _():
+            chain(0, c_near, side.at[c_near], side.at[c_near], partner).wait_recv()
+
+        @pl.when((c_right >= 0) & (c_right < chunks))
+        def _():
+            @pl.when(line > 0)
+            def _():
+                right_copy(c_right).wait_recv()
+
+            @pl.when(line < last)
+            def _():
+                to_right[c_right] = jnp.where(
+                    owner_line == line, here(c_right), rightward[c_right]
+                )
+                right_copy(c_right).start()
+
+        @pl.when((c_left >= 0) & (c_left < chunks))
+        def _():
+            @pl.when(line < last)
+            def _():
+                left_copy(c_left).wait_recv()
+
+            @pl.when(line > 0)
+            def _():
+                to_left[c_left] = jnp.where(owner_line == line, here(c_left), leftward[c_left])
+                left_copy(c_left).start()
+
+        @pl.when((c_far >= 0) & (c_far < chunks))
+        def _():
+            final[c_far] = jnp.where(
+                owner_line == line,
+                here(c_far),
+                jnp.where(owner_line < line, rightward[c_far], leftward[c_far]),
+            )
+            final_copy(c_far).start()
+            keep_copy(c_far).start()
+
+        upto = 2 + ((n - 2) * (t + 1)) // steps
+        while sent < upto:
+            send_block(sent)
+            sent += 1
+    for s in range(sent, n):
         send_block(s)
     own_block.wait()
     mine_state.wait()
-    mine_prefix.wait()
-    for copy in second_state + second_prefix + blocks:
+    for copy in sideways:
+        copy.wait_send()
+    for c in range(chunks):
+        keep_copy(c).wait()
+        final_copy(c).wait()
+
+        @pl.when(line < last)
+        def _():
+            right_copy(c).wait_send()
+
+        @pl.when(line > 0)
+        def _():
+            left_copy(c).wait_send()
+
+    for copy in second_state + blocks:
         copy.wait()
 
 
@@ -334,11 +399,10 @@
     n = send_kv.shape[0]
     any_spec = pl.BlockSpec(memory_space=pl.ANY)
     smem = pl.BlockSpec(memory_space=pltpu.SMEM)
-    rows, cols = prefix.shape[0] // n, states.shape[2] // n
-    two, height = states.shape[:2]
-    early = 1 + n // 4
+    piece = pltpu.VMEM(prefix.shape[1:], prefix.dtype)
+    chunks = prefix.shape[1]
     return pl.pallas_call(
-        lambda *refs: exchange_kernel(n, early, *refs),
+        lambda *refs: exchange_kernel(n, *refs),
         in_specs=[smem, smem, any_spec, any_spec, any_spec],
         out_specs=[any_spec] * 3,
         out_shape=[
@@ -347,17 +411,26 @@
             jax.ShapeDtypeStruct(send_kv.shape, send_kv.dtype),
         ],
         scratch_shapes=[
-            pltpu.VMEM((n, two, height, cols), states.dtype),
-            pltpu.VMEM((n, rows, prefix.shape[1]), prefix.dtype),
-            pltpu.VMEM((n, two, height, cols), states.dtype),
-            pltpu.VMEM((rows, prefix.shape[1]), prefix.dtype),
-            pltpu.SemaphoreType.DMA((5, n)),
-            pltpu.SemaphoreType.DMA((5, n)),
-            pltpu.SemaphoreType.DMA((5,)),
+            pltpu.VMEM(states.shape, states.dtype),
+            pltpu.VMEM(states.shape, states.dtype),
+        ]
+        + [piece] * 7
+        + [
+            pltpu.SemaphoreType.DMA((3, n)),
+            pltpu.SemaphoreType.DMA((3, n)),
+            pltpu.SemaphoreType.DMA((4, chunks)),
+            pltpu.SemaphoreType.DMA((4, chunks)),
+            pltpu.SemaphoreType.DMA((4 + chunks,)),
         ],
         compiler_params=pltpu.CompilerParams(collective_id=0, has_side_effects=True),
         name="exchange",
     )(owner_id, state_src, prefix, states, send_kv)
+
+
+def pack_states(ssm, conv, unit, width):
+    rows = ssm.shape[0] + conv.shape[0]
+    joined = jnp.pad(jnp.concatenate([ssm, conv], axis=0), ((0, -rows % unit), (0, 0)))
+    return jnp.swapaxes(joined.reshape(joined.shape[0], -1, width), 0, 1)
 
 
 def local(
@@ -390,27 +463,40 @@
     my_sources = lax.dynamic_index_in_dim(restore_src, own_index, 0, keepdims=False)
     picked = jnp.sum(jnp.where(restore_src == own_index, restore_blk, 0), axis=1)
     send_kv = jnp.take(pool_kv[0], picked, axis=0, mode="clip")
-    state_dim, taps = prefix_ssm.shape[1], prefix_conv.shape[1]
-    pad = -(state_dim + taps) % 8
-    states = jnp.stack(
-        [
-            jnp.pad(jnp.concatenate([ssm[0], conv[0]], axis=0), ((0, pad), (0, 0)))
-            for ssm, conv in ((prefix_ssm, prefix_conv), (pool_ssm, pool_conv))
-        ]
-    )
-    prefix, states, got_kv = exchange(owner_id, state_src, cached_lookup_pairs[0], states, send_kv)
+    n, width, channels = restore_src.shape[0], cached_lookup_pairs.shape[2], pool_ssm.shape[2]
+    length = cached_lookup_pairs.shape[1]
+    pool_states = pack_states(pool_ssm[0], pool_conv[0], 8, channels // n)
+    prefix_states = pack_states(prefix_ssm[0], prefix_conv[0], 16, width)
+    groups, height = prefix_states.shape[:2]
+    packed = jnp.concatenate([cached_lookup_pairs[0], prefix_states.reshape(-1, width)], axis=0)
+    shared, pool_states, got_kv = exchange(
+        owner_id, state_src, packed.reshape(2, CHUNKS, -1, width), pool_states, send_kv
+    )
+    shared = shared.reshape(packed.shape)
+    if groups == n:
+        offset = length // height
+        prefix_states = shared.reshape(-1, height, width)
+    else:
+        offset = 0
+        prefix_states = shared[length:].reshape(groups, height, width)
+        prefix_states = jnp.swapaxes(prefix_states, 0, 1).reshape(height, n, channels // n)
+        prefix_states = jnp.swapaxes(prefix_states, 0, 1)
     reading = (readers > 0).astype(jnp.int32)
-    signal, partial_bc = signal_call(reading, mamba_x, states, conv_w, conv_b[None], w_bc)
+    signal, partial_bc = signal_call(
+        reading, mamba_x, prefix_states, offset, pool_states, conv_w, conv_b[None], w_bc
+    )
     state_bc = lax.psum(partial_bc, "channel")
     mamba_out = scan_call(
-        reading, state_bc, signal, mamba_dt, mamba_z, dt_bias[None], a_log, bypass_gain[None], states
-    )
-    parts = prefix.shape[0] // block_len
-    prefix_blocks = prefix.reshape(parts, block_len, prefix.shape[1])
+        reading, state_bc, signal, mamba_dt, mamba_z, dt_bias[None], a_log, bypass_gain[None],
+        prefix_states, offset, pool_states
+    )
+    parts = length // block_len
     fresh_out = attend(
-        0, queries, prefix_blocks, lax.iota(jnp.int32, parts), reading * prefix.shape[0], new_kv
-    )
-    resumed_out = attend(1, queries, got_kv, my_sources, ctx_blocks * block_len, new_kv)
+        0, queries, shared, block_len, lax.iota(jnp.int32, parts), reading * length, new_kv
+    )
+    resumed_out = attend(
+        1, queries, got_kv.reshape(-1, width), block_len, my_sources, ctx_blocks * block_len, new_kv
+    )
     return (jnp.stack([fresh_out, resumed_out])[None], mamba_out)
 
 

time: 154 us -> 134 us (0.87)
  the two profiles are of different devices: /device:TPU:29 before, /device:TPU:21 now
where the time goes in v2:
time: 134 us; the launch traced here: 133 us
  Pallas kernels  114 us (85%)
  blocking collectives  6.42 us (5%)
  local copies, waits for them, and re-layouts  5.84 us (4%)
  other arithmetic  3.68 us (3%)
  between operations  2.67 us (2%)
    pallas_call x1, Pallas kernels, exchange(): pl.pallas_call(lambda *refs: exchange_kernel(n, *refs), in_specs=[smem, s...  90.6 us
    pallas_call x1, Pallas kernels, scan_call(): pl.pallas_call(scan_kernel, grid_spec=pltpu.PrefetchScalarGridSpec(num_sc...  9.82 us
    pallas_call x2, Pallas kernels, attend(): pl.pallas_call(lambda *refs: attend_kernel(parts, *refs), grid_spec=pltpu...  7.72 us
    psum x1, blocking collectives, local(): state_bc = lax.psum(partial_bc, 'channel')  6.42 us
    pallas_call x1, Pallas kernels, signal_call(): pl.pallas_call(signal_kernel, grid_spec=pltpu.PrefetchScalarGridSpec(num_...  6.36 us

profile of v2, /device:TPU:21, one launch (start us, length us, event | category | flops | bytes accessed | tf_op | source)
XLA Modules:
  0.0 133.1 jit_solution(8200300358105390266)
XLA Ops:
  0.6 0.0 copy-start
  0.6 0.8 select_reduce_fusion
  1.5 0.4 copy-done
  1.9 0.0 copy-start.4
  1.9 0.0 copy-start.6
  1.9 0.0 copy-start.1
  1.9 2.0 %gather_fusion = bf16[8,256,512]{2,1,0:T(8,128)(2,1)} fusion(bf16[4,256,512]{2,1,0:T(8,128)(2,1)S(1)} %bitcast.29, s32[1024]{0:T(1024)S(1)} %pad_clamp_fusion), kind=kCustom, calls=%fused_computation | custom fusion | bytes 4194336 | tf_op jit(solution)/shard_map/jit(_take)/gather | solution.py:465
  3.9 0.0 copy-start.5
  3.9 0.0 copy-start.7
  3.9 0.0 copy-done.4
  3.9 0.0 copy-done.6
  3.9 0.1 copy.31
  4.0 0.1 copy.27
  4.1 0.0 copy-done.1
  4.1 1.2 pad_maximum_fusion
  5.3 0.0 copy-done.5
  5.3 0.0 copy-done.7
  5.3 0.0 copy-start.3
  5.4 0.7 copy.33
  6.7 90.6 %exchange.1 = (bf16[2,4,160,512]{3,2,1,0:T(8,128)(2,1)}, bf16[8,24,512]{2,1,0:T(8,128)(2,1)}, bf16[8,256,512]{2,1,0:T(8,128)(2,1)}) custom-call(s32[1]{0:T(128)S(6)} %copy.34.refs_0_, s32[8]{0:T(128)} %refs_1_.1, bf16[2,4,160,512]{3,2,1,0:T(8,128)(2,1)} %bitcast.40, bf16[8,24,512]{2,1,0:T(8,128)(2,1)} %bitcast.46, bf16[8,256,512]{2,1,0:T(8,128)(2,1)} %gather_fusion), custom_call_target="tpu_custom_call" | custom-call | tf_op jit(solution)/shard_map/exchange/pallas_call | solution.py:404
  97.9 0.0 copy-done.3
  97.9 1.3 copy.29.wbc_ref
  99.3 6.4 %signal.1 = (f32[2,32,4096]{2,1,0:T(8,128)}, f32[2,32,32]{2,1,0:T(8,128)}) custom-call(s32[1]{0:T(128)S(6)} %convert_element_type.7.read_ref, bf16[1,2,32,4096]{3,2,1,0:T(8,128)(2,1)} %x_ref.1, bf16[40,32,512]{2,1,0:T(8,128)(2,1)} %bitcast.30, bf16[8,24,512]{2,1,0:T(8,128)(2,1)} %get-tuple-element.9.pool_ref, f32[4,4096]{1,0:T(4,128)} %w_ref.1, ...), custom_call_target="tpu_custom_call" | custom-call | tf_op jit(solution)/shard_map/signal/pallas_call | solution.py:132
  105.6 6.4 %psum.7.bc_ref = f32[2,32,32]{2,1,0:T(8,128)} all-reduce(f32[2,32,32]{2,1,0:T(8,128)} %get-tuple-element.10), channel_id=1, replica_groups=mesh['groups'=2,'replica'=8,'channel'=2] {'channel'}, use_global_device_ids=true, to_apply=%region_1.2 | all-reduce | flops 2048 | bytes 16384 | tf_op jit(solution)/shard_map/psum | solution.py:488
  112.0 0.0 copy-start.8
  112.0 9.8 %scan.1 = bf16[1,2,32,4096]{3,2,1,0:T(8,128)(2,1)} custom-call(s32[1]{0:T(128)S(6)} %convert_element_type.7.read_ref, f32[2,32,32]{2,1,0:T(8,128)} %psum.7.bc_ref, f32[2,32,4096]{2,1,0:T(8,128)} %get-tuple-element.11.sig_ref, bf16[1,2,32,4096]{3,2,1,0:T(8,128)(2,1)} %dt_ref.1, bf16[1,2,32,4096]{3,2,1,0:T(8,128)(2,1)} %z_ref.1, f32[1,4096]{1,0:T(1,128)} %bitcast.54, ...), custom_call_target="tpu_custom_call" | custom-call | tf_op jit(solution)/shard_map/scan/pallas_call | solution.py:210
  121.9 0.0 copy-done.8
  121.9 0.7 dynamic-slice_reduce_fusion.refs_0_
  123.2 3.8 %attend.3 = bf16[32,2048]{1,0:T(8,128)(2,1)} custom-call(s32[4]{0:T(128)} %dynamic-slice_reduce_fusion.refs_0_, s32[1]{0:T(128)S(6)} %mul.7.refs_1_, bf16[1,2,32,2048]{3,2,1,0:T(8,128)(2,1)} %refs_2_.3, bf16[2048,512]{1,0:T(8,128)(2,1)} %bitcast.36, bf16[2048,512]{1,0:T(8,128)(2,1)} %bitcast.37, bf16[2048,512]{1,0:T(8,128)(2,1)} %bitcast.38, ...), custom_call_target="tpu_custom_call" | custom-call | tf_op jit(solution)/shard_map/attend/pallas_call | solution.py:85
  127.0 0.5 iota.3.refs_0_
  127.5 0.0 copy-start.2
  127.5 3.9 %attend.2 = bf16[32,2048]{1,0:T(8,128)(2,1)} custom-call(s32[4]{0:T(128)} %iota.3.refs_0_, s32[1]{0:T(128)S(6)} %mul.6.refs_1_, bf16[1,2,32,2048]{3,2,1,0:T(8,128)(2,1)} %refs_2_.3, bf16[1280,512]{1,0:T(8,128)(2,1)} %bitcast.32, bf16[1280,512]{1,0:T(8,128)(2,1)} %bitcast.33, bf16[1280,512]{1,0:T(8,128)(2,1)} %bitcast.34, bf16[1280,512]{1,0:T(8,128)(2,1)} %bitcast.35, ...), custom_call_target="tpu_custom_call" | custom-call | tf_op jit(solution)/shard_map/attend/pallas_call | solution.py:85
  131.4 0.0 copy-done.2
  131.4 1.6 %maximum_bitcast_fusion = bf16[1,2,32,2048]{3,2,1,0:T(8,128)(2,1)} fusion(bf16[1,32,2048]{2,1,0:T(8,128)(2,1)S(1)} %bitcast.47, bf16[1,32,2048]{2,1,0:T(8,128)(2,1)} %bitcast.48), kind=kLoop, calls=%fused_computation.9 | loop fusion | flops 131072 | bytes 524288 | tf_op jit(solution)/shard_map/broadcast_in_dim | solution.py:500
  (3 shorter events, 0.1 us)
Async XLA Ops:
  0.6 1.3 copy-start
  1.9 2.0 %copy-start.4 = (bf16[1,16,4096]{2,1,0:T(8,128)(2,1)S(1)}, bf16[1,16,4096]{2,1,0:T(8,128)(2,1)}, u32[]{:S(2)}) copy-start(bf16[1,16,4096]{2,1,0:T(8,128)(2,1)} %param.26) | copy-start | bytes 393220
  1.9 2.0 %copy-start.6 = (bf16[1,3,4096]{2,1,0:T(4,128)(2,1)S(1)}, bf16[1,3,4096]{2,1,0:T(4,128)(2,1)}, u32[]{:S(2)}) copy-start(bf16[1,3,4096]{2,1,0:T(4,128)(2,1)} %param.27) | copy-start | bytes 73732
  1.9 2.2 %copy-start.1 = (bf16[1,1024,512]{2,1,0:T(8,128)(2,1)S(1)}, bf16[1,1024,512]{2,1,0:T(8,128)(2,1)}, u32[]{:S(2)}) copy-start(bf16[1,1024,512]{2,1,0:T(8,128)(2,1)} %param.25) | copy-start | bytes 3145732
  3.9 1.4 %copy-start.5 = (bf16[1,16,4096]{2,1,0:T(8,128)(2,1)S(1)}, bf16[1,16,4096]{2,1,0:T(8,128)(2,1)}, u32[]{:S(2)}) copy-start(bf16[1,16,4096]{2,1,0:T(8,128)(2,1)} %param.29) | copy-start | bytes 393220
  3.9 1.4 %copy-start.7 = (bf16[1,3,4096]{2,1,0:T(4,128)(2,1)S(1)}, bf16[1,3,4096]{2,1,0:T(4,128)(2,1)}, u32[]{:S(2)}) copy-start(bf16[1,3,4096]{2,1,0:T(4,128)(2,1)} %param.30) | copy-start | bytes 73732
  5.3 92.6 %copy-start.3 = (bf16[4096,32]{0,1:T(8,128)(2,1)S(1)}, bf16[4096,32]{0,1:T(8,128)(2,1)}, u32[]{:S(2)}) copy-start(bf16[4096,32]{0,1:T(8,128)(2,1)} %param.45) | copy-start | bytes 786436
  112.0 9.8 %copy-start.8 = (s32[8,4]{0,1:T(4,128)S(1)}, s32[8,4]{0,1:T(4,128)}, u32[]{:S(2)}) copy-start(s32[8,4]{0,1:T(4,128)} %param.33) | copy-start | bytes 388
  127.5 3.9 %copy-start.2 = (bf16[32,2048]{1,0:T(8,128)(2,1)S(1)}, bf16[32,2048]{1,0:T(8,128)(2,1)}, u32[]{:S(2)}) copy-start(bf16[32,2048]{1,0:T(8,128)(2,1)} %attend.3) | copy-start | bytes 393220

commit v3 on v2

--- a/solution.py
+++ b/solution.py
@@ -152,6 +152,7 @@
             jax.ShapeDtypeStruct((2, new_len, channels), jnp.float32),
             jax.ShapeDtypeStruct((2, new_len, cols), jnp.float32),
         ],
+        cost_estimate=pl.CostEstimate(flops=6_000_000_000, bytes_accessed=20_000_000, transcendentals=0),
         name="signal",
     )(reading, x, shared, pool, w, b, wbc)
 
@@ -232,12 +233,13 @@
             ],
         ),
         out_shape=jax.ShapeDtypeStruct((1, 2, new_len, channels), jnp.bfloat16),
+        cost_estimate=pl.CostEstimate(flops=10_000_000_000, bytes_accessed=30_000_000, transcendentals=0),
         name="scan",
     )(reading, bc, signal, dt, z, bias, alog, gain, shared, pool)
 
 
 def exchange_kernel(
-    n, owner_ref, holder_ref, prefix_ref, state_ref, send_ref, shared_ref, states_ref, got_ref,
+    n, owner_ref, holder_ref, prefix_ref, state_ref, shared_ref, states_ref,
     state_cand, state_send, own, side, rightward, leftward, to_right, to_left, final,
     sends, recvs, chain_sends, chain_recvs, local_sems
 ):
@@ -275,13 +277,11 @@
 
     own_prefix = pltpu.make_async_copy(prefix_ref.at[half], own, local_sems.at[0])
     own_state = pltpu.make_async_copy(state_ref.at[me], state_cand.at[me], local_sems.at[1])
-    own_block = pltpu.make_async_copy(send_ref.at[me], got_ref.at[me], local_sems.at[2])
     own_prefix.start()
     own_state.start()
-    own_block.start()
     pl.semaphore_wait(barrier, n - 1)
 
-    first_state, blocks, second_state, sideways = [], [], [], []
+    first_state, second_state, sideways = [], [], []
     for s in range(1, n):
         copy = spread(0, s, state_ref.at[lax.rem(me + s, n)], state_cand.at[me])
         copy.start()
@@ -291,12 +291,6 @@
         copy.start()
         sideways.append(copy)
 
-    def send_block(s):
-        copy = spread(1, s, send_ref.at[lax.rem(me + s, n)], got_ref.at[me])
-        copy.start()
-        blocks.append(copy)
-
-    send_block(1)
     own_state.wait()
     for copy in first_state:
         copy.wait()
@@ -327,7 +321,6 @@
 
     near, far = jnp.minimum(line, last - line), jnp.maximum(line, last - line)
     steps = chunks + length - 1
-    sent = 2
     for t in range(steps):
         c_near, c_right, c_left, c_far = t - near, t - line, t - (last - line), t - far
 
@@ -369,13 +362,6 @@
             final_copy(c_far).start()
             keep_copy(c_far).start()
 
-        upto = 2 + ((n - 2) * (t + 1)) // steps
-        while sent < upto:
-            send_block(sent)
-            sent += 1
-    for s in range(sent, n):
-        send_block(s)
-    own_block.wait()
     mine_state.wait()
     for copy in sideways:
         copy.wait_send()
@@ -391,24 +377,23 @@
         def _():
             left_copy(c).wait_send()
 
-    for copy in second_state + blocks:
+    for copy in second_state:
         copy.wait()
 
 
-def exchange(owner_id, state_src, prefix, states, send_kv):
-    n = send_kv.shape[0]
+def exchange(owner_id, state_src, prefix, states):
+    n = states.shape[0]
     any_spec = pl.BlockSpec(memory_space=pl.ANY)
     smem = pl.BlockSpec(memory_space=pltpu.SMEM)
     piece = pltpu.VMEM(prefix.shape[1:], prefix.dtype)
     chunks = prefix.shape[1]
     return pl.pallas_call(
         lambda *refs: exchange_kernel(n, *refs),
-        in_specs=[smem, smem, any_spec, any_spec, any_spec],
-        out_specs=[any_spec] * 3,
+        in_specs=[smem, smem, any_spec, any_spec],
+        out_specs=[any_spec] * 2,
         out_shape=[
             jax.ShapeDtypeStruct(prefix.shape, prefix.dtype),
             jax.ShapeDtypeStruct(states.shape, states.dtype),
-            jax.ShapeDtypeStruct(send_kv.shape, send_kv.dtype),
         ],
         scratch_shapes=[
             pltpu.VMEM(states.shape, states.dtype),
@@ -423,8 +408,9 @@
             pltpu.SemaphoreType.DMA((4 + chunks,)),
         ],
         compiler_params=pltpu.CompilerParams(collective_id=0, has_side_effects=True),
+        cost_estimate=pl.CostEstimate(flops=40_000_000_000, bytes_accessed=100_000_000, transcendentals=0),
         name="exchange",
-    )(owner_id, state_src, prefix, states, send_kv)
+    )(owner_id, state_src, prefix, states)
 
 
 def pack_states(ssm, conv, unit, width):
@@ -469,8 +455,11 @@
     prefix_states = pack_states(prefix_ssm[0], prefix_conv[0], 16, width)
     groups, height = prefix_states.shape[:2]
     packed = jnp.concatenate([cached_lookup_pairs[0], prefix_states.reshape(-1, width)], axis=0)
-    shared, pool_states, got_kv = exchange(
-        owner_id, state_src, packed.reshape(2, CHUNKS, -1, width), pool_states, send_kv
+    got_kv = lax.all_to_all(
+        send_kv[:, None], "replica", split_axis=0, concat_axis=1, tiled=True
+    )[0]
+    shared, pool_states = exchange(
+        owner_id, state_src, packed.reshape(2, CHUNKS, -1, width), pool_states
     )
     shared = shared.reshape(packed.shape)
     if groups == n:
@@ -494,6 +483,7 @@
     fresh_out = attend(
         0, queries, shared, block_len, lax.iota(jnp.int32, parts), reading * length, new_kv
     )
+    got_kv, mamba_out, fresh_out = lax.optimization_barrier((got_kv, mamba_out, fresh_out))
     resumed_out = attend(
         1, queries, got_kv.reshape(-1, width), block_len, my_sources, ctx_blocks * block_len, new_kv
     )

time: 134 us -> 134 us (level)
  the two profiles are of different devices: /device:TPU:21 before, /device:TPU:0 now
where the time goes in v3:
time: 134 us; the launch traced here: 133 us
  Pallas kernels  104 us (78%)
  local copies, waits for them, and re-layouts  8.23 us (6%)
  starting transfers between devices  7.44 us (6%)
  other arithmetic  5.63 us (4%)
  blocking collectives  4.64 us (3%)
  between operations  2.68 us (2%)
    pallas_call x1, Pallas kernels, exchange(): pl.pallas_call(lambda *refs: exchange_kernel(n, *refs), in_specs=[smem, s...  80.3 us
    pallas_call x1, Pallas kernels, scan_call(): pl.pallas_call(scan_kernel, grid_spec=pltpu.PrefetchScalarGridSpec(num_sc...  9.8 us
    pallas_call x2, Pallas kernels, attend(): pl.pallas_call(lambda *refs: attend_kernel(parts, *refs), grid_spec=pltpu...  7.74 us
    all_to_all x1, starting transfers between devices, local(): lax.all_to_all(send_kv[:, None], 'replica', split_axis=0, concat_axis=1,...  7.44 us
    pallas_call x1, Pallas kernels, signal_call(): pl.pallas_call(signal_kernel, grid_spec=pltpu.PrefetchScalarGridSpec(num_...  6.38 us
    psum x1, blocking collectives, local(): state_bc = lax.psum(partial_bc, 'channel')  4.64 us
    unnamed x16, local copies, waits for them, and re-layouts  4.2 us
  transfers between devices with their start and end apart: 1, of which 0 were waited for; matrix products, arithmetic and copies ran while one was open for 6% of the time, Pallas kernels for 75%

profile of v3, /device:TPU:0, one launch (start us, length us, event | category | flops | bytes accessed | tf_op | source)
XLA Modules:
  0.0 132.8 jit_solution(11970581970113007380)
XLA Ops:
  0.6 0.0 copy-start
  0.6 0.8 select_reduce_fusion
  1.5 0.4 copy-done
  1.9 2.0 %gather_fusion = bf16[8,256,512]{2,1,0:T(8,128)(2,1)} fusion(bf16[4,256,512]{2,1,0:T(8,128)(2,1)S(1)} %bitcast.31, s32[1024]{0:T(1024)S(1)} %pad_clamp_fusion), kind=kCustom, calls=%fused_computation | custom fusion | bytes 4194336 | tf_op jit(solution)/shard_map/jit(_take)/gather | solution.py:451
  3.9 0.0 copy-start.3
  3.9 0.0 copy-start.5
  3.9 0.0 copy-start.4
  3.9 7.4 %all-to-all-start = ((bf16[8,1,256,512]{3,2,1,0:T(8,128)(2,1)}), bf16[8,1,256,512]{3,2,1,0:T(8,128)(2,1)S(1)}, u32[]{:S(2)}, u32[]{:S(2)}) async-start(bf16[8,1,256,512]{3,2,1,0:T(8,128)(2,1)} %bitcast.42), calls=%async_computation | async-start | bytes 4194304 | tf_op jit(solution)/shard_map/all_to_all | solution.py:458
  11.4 0.0 copy-start.6
  11.4 0.0 copy-done.3
  11.4 0.0 copy-done.5
  11.4 0.1 copy.34
  11.5 0.1 copy.30
  11.6 0.0 copy-done.4
  11.6 0.8 fusion.5
  12.4 0.7 copy.36
  14.4 2.3 %copy.32.wbc_ref = bf16[4096,32]{1,0:T(8,128)(2,1)} copy(bf16[4096,32]{0,1:T(8,128)(2,1)} %param.45) | data formatting | bytes 524288 | tf_op args[22]
  16.7 0.0 copy-done.6
  16.7 0.7 dynamic-slice_reduce_fusion.refs_0_
  18.1 2.4 %pad_maximum_fusion = bf16[1280,512]{1,0:T(8,128)(2,1)} fusion(bf16[256,512]{1,0:T(8,128)(2,1)S(1)} %bitcast.44, bf16[1024,512]{1,0:T(8,128)(2,1)} %bitcast.45), kind=kLoop, calls=%fused_computation.1 | loop fusion | flops 2621440 | bytes 2621440 | tf_op jit(solution)/shard_map/concatenate | solution.py:457
  20.5 80.3 %exchange.1 = (bf16[2,4,160,512]{3,2,1,0:T(8,128)(2,1)}, bf16[8,24,512]{2,1,0:T(8,128)(2,1)}) custom-call(s32[1]{0:T(128)S(6)} %copy.37.refs_0_, s32[8]{0:T(128)} %refs_1_.1, bf16[2,4,160,512]{3,2,1,0:T(8,128)(2,1)} %bitcast.43, bf16[8,24,512]{2,1,0:T(8,128)(2,1)} %bitcast.51), custom_call_target="tpu_custom_call" | custom-call | flops 40000000000 | bytes 100000000 | tf_op jit(solution)/shard_map/exchange/pallas_call | solution.py:390
  100.8 0.5 iota.3.refs_0_
  101.3 3.8 %attend.2 = bf16[32,2048]{1,0:T(8,128)(2,1)} custom-call(s32[4]{0:T(128)} %iota.3.refs_0_, s32[1]{0:T(128)S(6)} %mul.6.refs_1_, bf16[1,2,32,2048]{3,2,1,0:T(8,128)(2,1)} %refs_2_.3, bf16[1280,512]{1,0:T(8,128)(2,1)} %bitcast.36, bf16[1280,512]{1,0:T(8,128)(2,1)} %bitcast.37, bf16[1280,512]{1,0:T(8,128)(2,1)} %bitcast.38, bf16[1280,512]{1,0:T(8,128)(2,1)} %bitcast.39, ...), custom_call_target="tpu_custom_call" | custom-call | tf_op jit(solution)/shard_map/attend/pallas_call | solution.py:85
  105.1 6.4 %signal.1 = (f32[2,32,4096]{2,1,0:T(8,128)}, f32[2,32,32]{2,1,0:T(8,128)}) custom-call(s32[1]{0:T(128)S(6)} %convert_element_type.7.read_ref, bf16[1,2,32,4096]{3,2,1,0:T(8,128)(2,1)} %x_ref.1, bf16[40,32,512]{2,1,0:T(8,128)(2,1)} %bitcast.40, bf16[8,24,512]{2,1,0:T(8,128)(2,1)} %get-tuple-element.10.pool_ref, f32[4,4096]{1,0:T(4,128)} %w_ref.1, ...), custom_call_target="tpu_custom_call" | custom-call | flops 6000000000 | bytes 20000000 | tf_op jit(solution)/shard_map/signal/pallas_call | solution.py:132
  111.5 4.6 %psum.7.bc_ref = f32[2,32,32]{2,1,0:T(8,128)} all-reduce(f32[2,32,32]{2,1,0:T(8,128)} %get-tuple-element.11), channel_id=1, replica_groups=mesh['groups'=2,'replica'=8,'channel'=2] {'channel'}, use_global_device_ids=true, to_apply=%region_1.2 | all-reduce | flops 2048 | bytes 16384 | tf_op jit(solution)/shard_map/psum | solution.py:477
  116.1 9.8 %scan.1 = bf16[1,2,32,4096]{3,2,1,0:T(8,128)(2,1)} custom-call(s32[1]{0:T(128)S(6)} %convert_element_type.7.read_ref, f32[2,32,32]{2,1,0:T(8,128)} %psum.7.bc_ref, f32[2,32,4096]{2,1,0:T(8,128)} %get-tuple-element.12.sig_ref, bf16[1,2,32,4096]{3,2,1,0:T(8,128)(2,1)} %dt_ref.1, bf16[1,2,32,4096]{3,2,1,0:T(8,128)(2,1)} %z_ref.1, f32[1,4096]{1,0:T(1,128)} %bitcast.57, ...), custom_call_target="tpu_custom_call" | custom-call | flops 10000000000 | bytes 30000000 | tf_op jit(solution)/shard_map/scan/pallas_call | solution.py:211
  125.9 0.0 all-to-all-done
  125.9 0.0 copy-start.1
  125.9 1.3 copy-done.1
  127.2 0.0 copy-start.2
  127.2 3.9 %attend.3 = bf16[32,2048]{1,0:T(8,128)(2,1)} custom-call(s32[4]{0:T(128)} %dynamic-slice_reduce_fusion.refs_0_, s32[1]{0:T(128)S(6)} %mul.7.refs_1_, bf16[1,2,32,2048]{3,2,1,0:T(8,128)(2,1)} %refs_2_.3, bf16[2048,512]{1,0:T(8,128)(2,1)} %bitcast.32, bf16[2048,512]{1,0:T(8,128)(2,1)} %bitcast.33, bf16[2048,512]{1,0:T(8,128)(2,1)} %bitcast.34, ...), custom_call_target="tpu_custom_call" | custom-call | tf_op jit(solution)/shard_map/attend/pallas_call | solution.py:85
  131.2 0.0 copy-done.2
  131.2 1.6 %maximum_bitcast_fusion = bf16[1,2,32,2048]{3,2,1,0:T(8,128)(2,1)} fusion(bf16[1,32,2048]{2,1,0:T(8,128)(2,1)} %bitcast.49, bf16[1,32,2048]{2,1,0:T(8,128)(2,1)S(1)} %bitcast.50), kind=kLoop, calls=%fused_computation.9 | loop fusion | flops 131072 | bytes 524288 | tf_op jit(solution)/shard_map/broadcast_in_dim | solution.py:490
  (2 shorter events, 0.0 us)
Async XLA Ops:
  0.6 1.3 copy-start
  3.9 7.5 %copy-start.3 = (bf16[1,16,4096]{2,1,0:T(8,128)(2,1)S(1)}, bf16[1,16,4096]{2,1,0:T(8,128)(2,1)}, u32[]{:S(2)}) copy-start(bf16[1,16,4096]{2,1,0:T(8,128)(2,1)} %param.26) | copy-start | bytes 393220
  3.9 7.5 %copy-start.5 = (bf16[1,3,4096]{2,1,0:T(4,128)(2,1)S(1)}, bf16[1,3,4096]{2,1,0:T(4,128)(2,1)}, u32[]{:S(2)}) copy-start(bf16[1,3,4096]{2,1,0:T(4,128)(2,1)} %param.27) | copy-start | bytes 73732
  3.9 7.7 %copy-start.4 = (bf16[1,16,4096]{2,1,0:T(8,128)(2,1)S(1)}, bf16[1,16,4096]{2,1,0:T(8,128)(2,1)}, u32[]{:S(2)}) copy-start(bf16[1,16,4096]{2,1,0:T(8,128)(2,1)} %param.29) | copy-start | bytes 393220
  3.9 122.0 %all-to-all-start = ((bf16[8,1,256,512]{3,2,1,0:T(8,128)(2,1)}), bf16[8,1,256,512]{3,2,1,0:T(8,128)(2,1)S(1)}, u32[]{:S(2)}, u32[]{:S(2)}) async-start(bf16[8,1,256,512]{3,2,1,0:T(8,128)(2,1)} %bitcast.42), calls=%async_computation | async-start | bytes 4194304 | tf_op jit(solution)/shard_map/all_to_all | solution.py:458
  11.4 5.4 %copy-start.6 = (s32[8,4]{0,1:T(4,128)S(1)}, s32[8,4]{0,1:T(4,128)}, u32[]{:S(2)}) copy-start(s32[8,4]{0,1:T(4,128)} %param.33) | copy-start | bytes 388
  125.9 1.3 %copy-start.1 = (bf16[8,1,256,512]{3,2,1,0:T(8,128)(2,1)}, bf16[8,1,256,512]{3,2,1,0:T(8,128)(2,1)S(1)}, u32[]{:S(2)}) copy-start(bf16[8,1,256,512]{3,2,1,0:T(8,128)(2,1)S(1)} %all-to-all-done) | copy-start | bytes 6291460
  127.2 4.0 %copy-start.2 = (bf16[32,2048]{1,0:T(8,128)(2,1)S(1)}, bf16[32,2048]{1,0:T(8,128)(2,1)}, u32[]{:S(2)}) copy-start(bf16[32,2048]{1,0:T(8,128)(2,1)} %attend.2) | copy-start | bytes 393220

commit v4 on v3

--- a/solution.py
+++ b/solution.py
@@ -455,12 +455,13 @@
     prefix_states = pack_states(prefix_ssm[0], prefix_conv[0], 16, width)
     groups, height = prefix_states.shape[:2]
     packed = jnp.concatenate([cached_lookup_pairs[0], prefix_states.reshape(-1, width)], axis=0)
+    shared, pool_states = exchange(
+        owner_id, state_src, packed.reshape(2, CHUNKS, -1, width), pool_states
+    )
+    send_kv, shared, pool_states = lax.optimization_barrier((send_kv, shared, pool_states))
     got_kv = lax.all_to_all(
         send_kv[:, None], "replica", split_axis=0, concat_axis=1, tiled=True
     )[0]
-    shared, pool_states = exchange(
-        owner_id, state_src, packed.reshape(2, CHUNKS, -1, width), pool_states
-    )
     shared = shared.reshape(packed.shape)
     if groups == n:
         offset = length // height

time: 134 us -> 114 us (0.85)
  Pallas kernels: 104 us -> 72.5 us
  waiting for transfers between devices: 0.01 us -> 17.7 us
  starting transfers between devices: 7.44 us -> 3.75 us
  local copies, waits for them, and re-layouts: 8.23 us -> 6.79 us
    pallas_call x1, Pallas kernels: 80.3 us -> 48.6 us  [exchange(): pl.pallas_call(lambda *refs: exchange_kernel(n, *refs), in_specs=[smem, s...]
    all_to_all x1, waiting for transfers between devices: 0.01 us -> 17.7 us  [local(): lax.all_to_all(send_kv[:, None], 'replica', split_axis=0, concat_axis=1,...]
    all_to_all x1, starting transfers between devices: 7.44 us -> 3.75 us  [local(): lax.all_to_all(send_kv[:, None], 'replica', split_axis=0, concat_axis=1,...]
    unnamed x16 -> x14, local copies, waits for them, and re-layouts: 4.2 us -> 2.78 us
  transfers between devices with their start and end apart: 1 -> 1, of which waited for: 0 -> 1; matrix products, arithmetic and copies ran while one was open for 6% -> 2% of each run, Pallas kernels for 75% -> 18%
where the time goes in v4:
time: 114 us
  Pallas kernels  72.5 us (64%)
  waiting for transfers between devices  17.7 us (16%)
  local copies, waits for them, and re-layouts  6.79 us (6%)
  other arithmetic  5.5 us (5%)
  blocking collectives  4.63 us (4%)
  starting transfers between devices  3.75 us (3%)
  between operations  2.68 us (2%)
    pallas_call x1, Pallas kernels, exchange(): pl.pallas_call(lambda *refs: exchange_kernel(n, *refs), in_specs=[smem, s...  48.6 us
    all_to_all x1, waiting for transfers between devices, local(): lax.all_to_all(send_kv[:, None], 'replica', split_axis=0, concat_axis=1,...  17.7 us
    pallas_call x1, Pallas kernels, scan_call(): pl.pallas_call(scan_kernel, grid_spec=pltpu.PrefetchScalarGridSpec(num_sc...  9.8 us
    pallas_call x2, Pallas kernels, attend(): pl.pallas_call(lambda *refs: attend_kernel(parts, *refs), grid_spec=pltpu...  7.73 us
    pallas_call x1, Pallas kernels, signal_call(): pl.pallas_call(signal_kernel, grid_spec=pltpu.PrefetchScalarGridSpec(num_...  6.38 us
    psum x1, blocking collectives, local(): state_bc = lax.psum(partial_bc, 'channel')  4.63 us
    all_to_all x1, starting transfers between devices, local(): lax.all_to_all(send_kv[:, None], 'replica', split_axis=0, concat_axis=1,...  3.75 us
    unnamed x14, local copies, waits for them, and re-layouts  2.78 us
  transfers between devices with their start and end apart: 1, of which 1 were waited for; matrix products, arithmetic and copies ran while one was open for 2% of the time, Pallas kernels for 18%

profile of v4, /device:TPU:0, one launch (start us, length us, event | category | flops | bytes accessed | tf_op | source)
XLA Modules:
  0.0 113.5 jit_solution(2775741532891002294)
XLA Ops:
  0.6 0.0 copy-start
  0.6 0.8 select_reduce_fusion
  1.5 1.0 fusion.4
  2.4 0.1 copy.34
  2.5 0.1 copy.30
  2.6 1.0 fusion.5
  3.6 0.7 copy.36
  4.9 0.0 copy-done
  4.9 0.0 copy-start.2
  4.9 2.0 %gather_fusion = bf16[8,256,512]{2,1,0:T(8,128)(2,1)} fusion(bf16[4,256,512]{2,1,0:T(8,128)(2,1)S(1)} %bitcast.31, s32[1024]{0:T(1024)S(1)} %pad_clamp_fusion), kind=kCustom, calls=%fused_computation | custom fusion | bytes 4194336 | tf_op jit(solution)/shard_map/jit(_take)/gather | solution.py:451
  6.9 0.0 copy-done.2
  6.9 1.2 %pad_maximum_fusion = bf16[1280,512]{1,0:T(8,128)(2,1)} fusion(bf16[256,512]{1,0:T(8,128)(2,1)S(1)} %bitcast.44, bf16[1024,512]{1,0:T(8,128)(2,1)S(1)} %bitcast.45), kind=kLoop, calls=%fused_computation.1 | loop fusion | flops 2621440 | bytes 2621440 | tf_op jit(solution)/shard_map/concatenate | solution.py:457
  8.1 48.6 %exchange.1 = (bf16[2,4,160,512]{3,2,1,0:T(8,128)(2,1)}, bf16[8,24,512]{2,1,0:T(8,128)(2,1)}) custom-call(s32[1]{0:T(128)S(6)} %copy.37.refs_0_, s32[8]{0:T(128)} %refs_1_.1, bf16[2,4,160,512]{3,2,1,0:T(8,128)(2,1)} %bitcast.43, bf16[8,24,512]{2,1,0:T(8,128)(2,1)} %bitcast.51), custom_call_target="tpu_custom_call" | custom-call | flops 40000000000 | bytes 100000000 | tf_op jit(solution)/shard_map/exchange/pallas_call | solution.py:390
  56.7 0.0 copy-start.4
  56.7 0.0 copy-start.5
  56.7 3.7 %all-to-all-start = ((bf16[8,1,256,512]{3,2,1,0:T(8,128)(2,1)}), bf16[8,1,256,512]{3,2,1,0:T(8,128)(2,1)S(1)}, u32[]{:S(2)}, u32[]{:S(2)}) async-start(bf16[8,1,256,512]{3,2,1,0:T(8,128)(2,1)} %bitcast.42), calls=%async_computation | async-start | bytes 4194304 | tf_op jit(solution)/shard_map/all_to_all | solution.py:462
  61.1 0.0 copy-done.4
  61.1 1.3 %copy.32.wbc_ref = bf16[4096,32]{1,0:T(8,128)(2,1)} copy(bf16[4096,32]{0,1:T(8,128)(2,1)S(1)} %copy-done.4) | data formatting | bytes 524288 | tf_op args[22]
  62.5 0.0 copy-done.5
  62.5 0.7 dynamic-slice_reduce_fusion.refs_0_
  63.8 0.5 iota.3.refs_0_
  64.3 3.8 %attend.2 = bf16[32,2048]{1,0:T(8,128)(2,1)} custom-call(s32[4]{0:T(128)} %iota.3.refs_0_, s32[1]{0:T(128)S(6)} %mul.6.refs_1_, bf16[1,2,32,2048]{3,2,1,0:T(8,128)(2,1)} %refs_2_.3, bf16[1280,512]{1,0:T(8,128)(2,1)} %bitcast.36, bf16[1280,512]{1,0:T(8,128)(2,1)} %bitcast.37, bf16[1280,512]{1,0:T(8,128)(2,1)} %bitcast.38, bf16[1280,512]{1,0:T(8,128)(2,1)} %bitcast.39, ...), custom_call_target="tpu_custom_call" | custom-call | tf_op jit(solution)/shard_map/attend/pallas_call | solution.py:85
  68.1 6.4 %signal.1 = (f32[2,32,4096]{2,1,0:T(8,128)}, f32[2,32,32]{2,1,0:T(8,128)}) custom-call(s32[1]{0:T(128)S(6)} %convert_element_type.7.read_ref, bf16[1,2,32,4096]{3,2,1,0:T(8,128)(2,1)} %x_ref.1, bf16[40,32,512]{2,1,0:T(8,128)(2,1)} %bitcast.40, bf16[8,24,512]{2,1,0:T(8,128)(2,1)} %get-tuple-element.16.pool_ref, f32[4,4096]{1,0:T(4,128)} %w_ref.1, ...), custom_call_target="tpu_custom_call" | custom-call | flops 6000000000 | bytes 20000000 | tf_op jit(solution)/shard_map/signal/pallas_call | solution.py:132
  74.5 4.6 %psum.7.bc_ref = f32[2,32,32]{2,1,0:T(8,128)} all-reduce(f32[2,32,32]{2,1,0:T(8,128)} %get-tuple-element.17), channel_id=1, replica_groups=mesh['groups'=2,'replica'=8,'channel'=2] {'channel'}, use_global_device_ids=true, to_apply=%region_1.2 | all-reduce | flops 2048 | bytes 16384 | tf_op jit(solution)/shard_map/psum | solution.py:478
  79.1 9.8 %scan.1 = bf16[1,2,32,4096]{3,2,1,0:T(8,128)(2,1)} custom-call(s32[1]{0:T(128)S(6)} %convert_element_type.7.read_ref, f32[2,32,32]{2,1,0:T(8,128)} %psum.7.bc_ref, f32[2,32,4096]{2,1,0:T(8,128)} %get-tuple-element.18.sig_ref, bf16[1,2,32,4096]{3,2,1,0:T(8,128)(2,1)} %dt_ref.1, bf16[1,2,32,4096]{3,2,1,0:T(8,128)(2,1)} %z_ref.1, f32[1,4096]{1,0:T(1,128)} %bitcast.57, ...), custom_call_target="tpu_custom_call" | custom-call | flops 10000000000 | bytes 30000000 | tf_op jit(solution)/shard_map/scan/pallas_call | solution.py:211
  88.9 17.7 %all-to-all-done = bf16[8,1,256,512]{3,2,1,0:T(8,128)(2,1)S(1)} async-done(((bf16[8,1,256,512]{3,2,1,0:T(8,128)(2,1)}), bf16[8,1,256,512]{3,2,1,0:T(8,128)(2,1)S(1)}, u32[]{:S(2)}, u32[]{:S(2)}) %all-to-all-start) | async-done | bytes 2097184 | tf_op jit(solution)/shard_map/all_to_all | solution.py:462
  106.6 0.0 copy-start.1
  106.6 1.3 %copy-done.1 = bf16[8,1,256,512]{3,2,1,0:T(8,128)(2,1)} copy-done((bf16[8,1,256,512]{3,2,1,0:T(8,128)(2,1)}, bf16[8,1,256,512]{3,2,1,0:T(8,128)(2,1)S(1)}, u32[]{:S(2)}) %copy-start.1) | copy-done | bytes 2097176
  108.0 0.0 copy-start.3
  108.0 3.9 %attend.3 = bf16[32,2048]{1,0:T(8,128)(2,1)} custom-call(s32[4]{0:T(128)} %dynamic-slice_reduce_fusion.refs_0_, s32[1]{0:T(128)S(6)} %mul.7.refs_1_, bf16[1,2,32,2048]{3,2,1,0:T(8,128)(2,1)} %refs_2_.3, bf16[2048,512]{1,0:T(8,128)(2,1)} %bitcast.32, bf16[2048,512]{1,0:T(8,128)(2,1)} %bitcast.33, bf16[2048,512]{1,0:T(8,128)(2,1)} %bitcast.34, ...), custom_call_target="tpu_custom_call" | custom-call | tf_op jit(solution)/shard_map/attend/pallas_call | solution.py:85
  111.9 0.0 copy-done.3
  111.9 1.6 %maximum_bitcast_fusion = bf16[1,2,32,2048]{3,2,1,0:T(8,128)(2,1)} fusion(bf16[1,32,2048]{2,1,0:T(8,128)(2,1)} %bitcast.49, bf16[1,32,2048]{2,1,0:T(8,128)(2,1)S(1)} %bitcast.50), kind=kLoop, calls=%fused_computation.9 | loop fusion | flops 131072 | bytes 524288 | tf_op jit(solution)/shard_map/broadcast_in_dim | solution.py:491
  (1 shorter events, 0.0 us)
Async XLA Ops:
  0.6 4.3 %copy-start = (bf16[1,4,256,512]{3,2,1,0:T(8,128)(2,1)S(1)}, bf16[1,4,256,512]{3,2,1,0:T(8,128)(2,1)}, u32[]{:S(2)}) copy-start(bf16[1,4,256,512]{3,2,1,0:T(8,128)(2,1)} %param.28) | copy-start | bytes 3145732
  4.9 2.0 %copy-start.2 = (bf16[1,1024,512]{2,1,0:T(8,128)(2,1)S(1)}, bf16[1,1024,512]{2,1,0:T(8,128)(2,1)}, u32[]{:S(2)}) copy-start(bf16[1,1024,512]{2,1,0:T(8,128)(2,1)} %param.25) | copy-start | bytes 3145732
  56.7 4.4 %copy-start.4 = (bf16[4096,32]{0,1:T(8,128)(2,1)S(1)}, bf16[4096,32]{0,1:T(8,128)(2,1)}, u32[]{:S(2)}) copy-start(bf16[4096,32]{0,1:T(8,128)(2,1)} %param.45) | copy-start | bytes 786436
  56.7 5.8 %copy-start.5 = (s32[8,4]{0,1:T(4,128)S(1)}, s32[8,4]{0,1:T(4,128)}, u32[]{:S(2)}) copy-start(s32[8,4]{0,1:T(4,128)} %param.33) | copy-start | bytes 388
  56.7 49.9 %all-to-all-start = ((bf16[8,1,256,512]{3,2,1,0:T(8,128)(2,1)}), bf16[8,1,256,512]{3,2,1,0:T(8,128)(2,1)S(1)}, u32[]{:S(2)}, u32[]{:S(2)}) async-start(bf16[8,1,256,512]{3,2,1,0:T(8,128)(2,1)} %bitcast.42), calls=%async_computation | async-start | bytes 4194304 | tf_op jit(solution)/shard_map/all_to_all | solution.py:462
  106.6 1.3 %copy-start.1 = (bf16[8,1,256,512]{3,2,1,0:T(8,128)(2,1)}, bf16[8,1,256,512]{3,2,1,0:T(8,128)(2,1)S(1)}, u32[]{:S(2)}) copy-start(bf16[8,1,256,512]{3,2,1,0:T(8,128)(2,1)S(1)} %all-to-all-done) | copy-start | bytes 6291460
  108.0 3.9 %copy-start.3 = (bf16[32,2048]{1,0:T(8,128)(2,1)S(1)}, bf16[32,2048]{1,0:T(8,128)(2,1)}, u32[]{:S(2)}) copy-start(bf16[32,2048]{1,0:T(8,128)(2,1)} %attend.2) | copy-start | bytes 393220
